TPU v7x, 512 devices: a whole 4x8x8 slice. The times are simulated.
512 devices in a mesh: group: 16 (over y_lo, x), sub: 32 (over z, y_hi, core).
Axes of the slice: x: 4, y: 8 (y_hi: 2, y_lo: 4; y = y_hi * 4 + y_lo), z: 8, core: 2. Of those that a mesh axis runs over, the one named last changes fastest.
Arguments:
- initial_condition: bfloat16 [16, 64, 192, 384], P('group', None, 'sub'), may hold values from -6 to 6
- enc_weight: bfloat16 [128, 64], replicated, may hold values from -0.75 to 0.75
- spec_weight: bfloat16 [2, 2, 128, 128], replicated, may hold values from -0.375 to 0.375
- norm_gain: float32 [2, 128], replicated, may hold values from 0.25 to 1.75
- up_weight: bfloat16 [2, 256, 128], replicated, may hold values from -0.5 to 0.5
- down_weight: bfloat16 [2, 128, 256], replicated, may hold values from -0.375 to 0.375
- output_projection_matrix: bfloat16 [64, 128], replicated, may hold values from -0.5 to 0.5
- obs_pos: int32 [32, 16, 512], P('sub', 'group'), may hold values from 0 to 9215
- obs_count: int32 [32, 16], P('sub', 'group'), may hold values from 64 to 512, as said below
- obs_value: float32 [32, 16, 512], P('sub', 'group'), may hold values from -6 to 6
- obs_var: float32 [32, 16, 512], P('sub', 'group'), may hold values from 0.25 to 4
- modulation: float32 [32, 16, 16, 144], P('sub', 'group'), may hold values from -6 to 6
Outputs:
- analysis: bfloat16 [32, 16, 16, 9216], P('sub', 'group')
Inputs may be any that keep to these rules, and one draw needn't show every extreme that they name: `obs_count`: at least one tile holds exactly 512 observations.
All inputs are finite; a program needn't handle non-finite values.
Results may differ from a plain program's by a relative error of at most 0.04.
Values may be sent and summed in bfloat16 or wider, within the bound.
A program may use at most 64 MiB of HBM per device.

v0:
```python
import math

import jax
import jax.numpy as jnp
from jax import lax
from jax.sharding import PartitionSpec as P

LMAX = 192
MMAX = 192
LAYERS = 2


def product(pattern, first_operand, second_operand):
    return jnp.einsum(pattern, first_operand, second_operand, preferred_element_type=jnp.float32)


def fourier_tables(lon_count, mode_count):
    lon_points = jnp.arange(lon_count, dtype=jnp.int32)
    mode_values = jnp.arange(mode_count, dtype=jnp.int32)
    phase_index = mode_values[:, None] * lon_points[None, :] % lon_count
    angles = phase_index.astype(jnp.float32) * (2.0 * math.pi / lon_count)
    cosine_values = jnp.cos(angles)
    sine_values = jnp.sin(angles)
    forward = jnp.concatenate([cosine_values, -sine_values], axis=0).T / lon_count
    twofold = jnp.where(mode_values == 0, 1.0, 2.0).astype(jnp.float32)[:, None]
    inverse = jnp.stack([twofold * cosine_values, -twofold * sine_values], axis=0)
    return (forward.astype(jnp.bfloat16), inverse.astype(jnp.bfloat16))


def sphere_tables(mode_ids, degree_count, lat_count):
    colatitude = (jnp.arange(lat_count, dtype=jnp.float32) + 0.5) * (math.pi / lat_count)
    cosine_values = jnp.cos(colatitude)[None, :]
    sine_values = jnp.sin(colatitude)[None, :]
    order_value = mode_ids.astype(jnp.float32)[:, None]
    log_start = 0.5 * (
        jnp.log((2.0 * order_value + 1.0) / (4.0 * math.pi))
        + jax.scipy.special.gammaln(order_value + 0.5)
        - jax.scipy.special.gammaln(order_value + 1.0)
        - 0.5 * math.log(math.pi)
    ) + order_value * jnp.log(sine_values)
    diagonal_start = jnp.exp(log_start)

    def advance(carried, degree):
        previous, earlier = carried
        degree_value = degree.astype(jnp.float32)
        upper_factor = jnp.sqrt(
            (4.0 * degree_value * degree_value - 1.0)
            / jnp.maximum(degree_value * degree_value - order_value * order_value, 1.0)
        )
        lower_factor = jnp.sqrt(
            jnp.maximum(
                (degree_value - 1.0) * (degree_value - 1.0) - order_value * order_value, 0.0
            )
            / jnp.maximum(4.0 * (degree_value - 1.0) * (degree_value - 1.0) - 1.0, 1.0)
        )
        recursion = upper_factor * (cosine_values * previous - lower_factor * earlier)
        next_value = jnp.where(
            degree_value < order_value,
            0.0,
            jnp.where(
                degree_value == order_value,
                diagonal_start,
                jnp.where(
                    degree_value == order_value + 1.0,
                    cosine_values * jnp.sqrt(2.0 * order_value + 3.0) * diagonal_start,
                    recursion,
                ),
            ),
        )
        return ((next_value, previous), next_value)

    zero_rows = jnp.zeros((mode_ids.shape[0], lat_count), jnp.float32)
    _, legendre_rows = lax.scan(
        advance, (zero_rows, zero_rows), jnp.arange(degree_count, dtype=jnp.int32)
    )
    legendre_rows = jnp.transpose(legendre_rows, (1, 0, 2))
    quadrature = 2.0 * math.pi * (math.pi / lat_count) * jnp.sin(colatitude)
    forward = (legendre_rows * quadrature[None, None, :]).astype(jnp.bfloat16)
    inverse = jnp.transpose(legendre_rows, (0, 2, 1)).astype(jnp.bfloat16)
    return (forward, inverse)


def encode(member_state, enc_weight):
    return product("cv,bvyn->bcyn", enc_weight, member_state).astype(jnp.bfloat16)


def to_modes(latent_features, forward_dft):
    zonal = product("bcyn,nk->bcyk", latent_features, forward_dft).astype(jnp.bfloat16)
    return zonal.reshape(
        latent_features.shape[0],
        latent_features.shape[1],
        latent_features.shape[2],
        2,
        forward_dft.shape[1] // 2,
    )


def spectral(columns, legendre_fwd, legendre_inv, mixing):
    coefficients = product("bcyrm,mly->bclrm", columns, legendre_fwd).astype(jnp.bfloat16)
    real_part = product("oc,bclrm->bolrm", mixing[0], coefficients)
    imag_part = product("oc,bclrm->bolrm", mixing[1], coefficients)
    mixed_modes = jnp.stack(
        [
            real_part[:, :, :, 0] - imag_part[:, :, :, 1],
            real_part[:, :, :, 1] + imag_part[:, :, :, 0],
        ],
        axis=3,
    ).astype(jnp.bfloat16)
    return product("bclrm,myl->bcyrm", mixed_modes, legendre_inv).astype(jnp.bfloat16)


def finish(latent_features, back, inverse_dft, gain, w_up, w_down):
    summed = latent_features.astype(jnp.float32) + product("bcyrm,rmn->bcyn", back, inverse_dft)
    centered = summed - jnp.mean(summed, axis=1, keepdims=True)
    spread = jnp.mean(centered * centered, axis=1, keepdims=True)
    normed = (centered * lax.rsqrt(spread + 1e-05) * gain[None, :, None, None]).astype(jnp.bfloat16)
    lifted = jax.nn.gelu(product("hc,bcyn->bhyn", w_up, normed), approximate=False).astype(
        jnp.bfloat16
    )
    return (summed + product("ch,bhyn->bcyn", w_down, lifted)).astype(jnp.bfloat16)


def project_features_out(member_state, latent_features, output_projection_matrix):
    return (
        member_state.astype(jnp.float32)
        + product("vc,bcyn->bvyn", output_projection_matrix, latent_features)
    ).astype(jnp.bfloat16)


def prepare(patch_realization_fields, positions, values, obs_total, modulation):
    background = patch_realization_fields.astype(jnp.float32)
    member_count = background.shape[0]
    ensemble_mean = jnp.sum(background, axis=0) / member_count
    perturb = background - ensemble_mean[None, :]
    tile_grid_cells = modulation.shape[1]
    is_valid = (jnp.arange(positions.shape[0], dtype=jnp.int32) < obs_total).astype(jnp.float32)
    picked = jnp.take(perturb, positions, axis=1).T
    observed = jnp.take(background, positions, axis=1).T
    mode_at_obs = jnp.take(modulation, positions % tile_grid_cells, axis=1).T
    anomaly_scale = 1.0 / math.sqrt(member_count - 1)
    anomalies = (
        (is_valid * anomaly_scale)[:, None, None] * picked[:, :, None] * mode_at_obs[:, None, :]
    ).reshape(positions.shape[0], -1)
    innovation = is_valid[:, None] * (values[:, None] - observed)
    return (background, perturb, anomalies, innovation, anomaly_scale)


def cholesky_solve(system, right_side):
    factor = jnp.linalg.cholesky(system)
    partial_solve = jax.scipy.linalg.solve_triangular(factor, right_side, lower=True)
    return jax.scipy.linalg.solve_triangular(factor, partial_solve, lower=True, trans=1)


def weights_observed(anomalies, innovation, variances):
    system = jnp.dot(anomalies, anomalies.T, precision=lax.Precision.HIGHEST) + jnp.diag(variances)
    return jnp.dot(anomalies.T, cholesky_solve(system, innovation), precision=lax.Precision.HIGHEST)


def apply_update(background, perturb, coupling, modulation, anomaly_scale):
    member_count = background.shape[0]
    mode_count = modulation.shape[0]
    variable_count = perturb.shape[1] // modulation.shape[1]
    coupling_table = coupling.reshape(member_count, mode_count, member_count)

    def add_mode(mode_index, summed_terms):
        mode_block = lax.dynamic_index_in_dim(coupling_table, mode_index, axis=1, keepdims=False)
        mode_row = jnp.tile(
            lax.dynamic_index_in_dim(modulation, mode_index, axis=0, keepdims=False), variable_count
        )
        return summed_terms + mode_row[None, :] * jnp.dot(
            mode_block.T, perturb, precision=lax.Precision.HIGHEST
        )

    summed_terms = lax.fori_loop(0, mode_count, add_mode, jnp.zeros_like(perturb))
    return (background + anomaly_scale * summed_terms).astype(jnp.bfloat16)


def shards(
    initial_condition,
    enc_weight,
    spec_weight,
    norm_gain,
    up_weight,
    down_weight,
    output_projection_matrix,
    obs_pos,
    obs_count,
    obs_value,
    obs_var,
    modulation,
):
    groups_count = lax.axis_size("group")
    sub_count = lax.axis_size("sub")
    members_per_device, variable_count, lat_dev, lon_count = initial_condition.shape
    lat_total = lat_dev * sub_count
    mode_dev = MMAX // sub_count
    forward_dft, inverse_dft = fourier_tables(lon_count, MMAX)
    mode_ids = lax.axis_index("sub") * mode_dev + jnp.arange(mode_dev, dtype=jnp.int32)
    legendre_fwd, legendre_inv = sphere_tables(mode_ids, LMAX, lat_total)
    latent_features = encode(initial_condition, enc_weight)
    member_rows = [latent_features]
    for layer_index in range(LAYERS):
        hidden_rows = member_rows[0]
        columns = (
            lambda operand: lax.all_to_all(operand, "sub", split_axis=4, concat_axis=2, tiled=True)
        )(to_modes(hidden_rows, forward_dft))
        back = (
            lambda operand: lax.all_to_all(operand, "sub", split_axis=2, concat_axis=4, tiled=True)
        )(spectral(columns, legendre_fwd, legendre_inv, spec_weight[layer_index]))
        member_rows[0] = finish(
            hidden_rows,
            back,
            inverse_dft,
            norm_gain[layer_index],
            up_weight[layer_index],
            down_weight[layer_index],
        )
    latent_features = member_rows[0]
    predicted_realizations = project_features_out(
        initial_condition, latent_features, output_projection_matrix
    )
    tile_grid_cells = lat_dev * lon_count // groups_count
    copy_finished = predicted_realizations.reshape(
        members_per_device, variable_count, groups_count, tile_grid_cells
    )
    arrived = lax.all_to_all(copy_finished, "group", split_axis=2, concat_axis=0, tiled=True)
    patch_realization_fields = arrived.reshape(
        members_per_device * groups_count, variable_count * tile_grid_cells
    )
    mode_values = modulation[0, 0]
    background, perturb, anomalies, innovation, anomaly_scale = prepare(
        patch_realization_fields, obs_pos[0, 0], obs_value[0, 0], obs_count[0, 0], mode_values
    )
    coupling = weights_observed(anomalies, innovation, obs_var[0, 0])
    result = apply_update(background, perturb, coupling, mode_values, anomaly_scale)
    return result[None, None]


def solution(mesh):
    return jax.shard_map(
        shards,
        mesh=mesh,
        in_specs=(
            P("group", None, "sub", None),
            P(),
            P(),
            P(),
            P(),
            P(),
            P(),
            P("sub", "group", None),
            P("sub", "group"),
            P("sub", "group", None),
            P("sub", "group", None),
            P("sub", "group", None, None),
        ),
        out_specs=P("sub", "group", None, None),
        check_vma=False,
    )
```

profile of v0, /device:TPU:56, one launch (start us, length us, event | category | flops | bytes accessed | tf_op | source)
XLA Modules:
  0.0 745.8 jit_solution(283269393110057710)
XLA Ops:
  4.8 15.8 %all-to-all-start = ((bf16[1,128,6,2,192]{1,3,2,0,4:T(2,128)(2,1)}), bf16[1,128,6,2,192]{1,3,2,0,4:T(2,128)(2,1)S(1)}, u32[]{:S(2)}, u32[]{:S(2)}) async-start(bf16[1,128,6,2,192]{1,3,2,0,4:T(2,128)(2,1)} %copy.123), calls=%async_computation | async-start | bytes 1179648 | tf_op jit(solution)/shard_map/all_to_all | solution.py:205
  20.9 400.1 %while.38 = (s32[]{:T(128)}, f32[6,192]{1,0:T(8,128)S(1)}, f32[6,192]{1,0:T(8,128)S(1)}, f32[192,6,192]{2,1,0:T(8,128)}, s32[192]{0:T(256)S(1)}, /*index=5*/s32[...) while((s32[]{:T(128)}, f32[6,192]{1,0:T(8,128)S(1)}, ...), condition=%wide.region_1.2_spmd.clone.clone.clone.clone, body=%wide.region_0.1_spmd.clone.clone.clone.clone.sunk | while | flops 14354 | bytes 29991 | solution.py:73
  428.8 12.5 %all-to-all-start.1 = ((bf16[1,128,192,2,6]{1,3,4,0,2:T(2,128)(2,1)}), bf16[1,128,192,2,6]{1,3,4,0,2:T(2,128)(2,1)S(1)}, u32[]{:S(2)}, u32[]{:S(2)}) async-start(bf16[1,128,192,2,6]{1,3,4,0,2:T(2,128)(2,1)} %copy.132), calls=%async_computation.1 | async-start | bytes 1179648 | tf_op jit(solution)/shard_map/all_to_all | solution.py:208
  442.7 17.3 %all-to-all-done.1 = bf16[1,128,192,2,6]{1,3,4,0,2:T(2,128)(2,1)S(1)} async-done(((bf16[1,128,192,2,6]{1,3,4,0,2:T(2,128)(2,1)}), bf16[1,128,192,2,6]{1,3,4,0,2:T(2,128)(2,1)S(1)}, u32[]{:S(2)}, u32[]{:S(2)}) %all-to-all-start.1) | async-done | bytes 589856 | tf_op jit(solution)/shard_map/all_to_all | solution.py:208
  461.2 6.6 fusion.51
  469.3 27.0 %all_to_all.69 = bf16[1,128,6,2,192]{1,3,2,0,4:T(2,128)(2,1)S(1)} all-to-all(bf16[1,128,6,2,192]{1,3,2,0,4:T(2,128)(2,1)S(1)} %copy.138), channel_id=1, replica_groups=mesh['group'=16,'sub'=32] {'sub'}, dimensions={4} | all-to-all | bytes 1179648 | tf_op jit(solution)/shard_map/all_to_all | solution.py:205
  500.6 7.4 all-to-all-start.3
  510.1 17.0 %all-to-all-done.3 = bf16[1,128,192,2,6]{1,3,4,0,2:T(2,128)(2,1)S(1)} async-done(((bf16[1,128,192,2,6]{1,3,4,0,2:T(2,128)(2,1)}), bf16[1,128,192,2,6]{1,3,4,0,2:T(2,128)(2,1)S(1)}, u32[]{:S(2)}, u32[]{:S(2)}) %all-to-all-start.3) | async-done | bytes 589856 | tf_op jit(solution)/shard_map/all_to_all | solution.py:208
  528.3 6.7 fusion.57
  537.4 10.1 %all-to-all-start.4 = ((bf16[1,64,16,144]{3,1,0,2:T(8,128)(2,1)}), bf16[1,64,16,144]{3,1,0,2:T(8,128)(2,1)S(1)}, u32[]{:S(2)}, u32[]{:S(2)}) async-start(bf16[1,64,16,144]{3,1,0,2:T(8,128)(2,1)} %copy.153), calls=%async_computation.4 | async-start | bytes 1048576 | tf_op jit(solution)/shard_map/all_to_all | solution.py:226
  547.5 11.9 %all-to-all-done.4 = bf16[1,64,16,144]{3,1,0,2:T(8,128)(2,1)S(1)} async-done(((bf16[1,64,16,144]{3,1,0,2:T(8,128)(2,1)}), bf16[1,64,16,144]{3,1,0,2:T(8,128)(2,1)S(1)}, u32[]{:S(2)}, u32[]{:S(2)}) %all-to-all-start.4) | async-done | bytes 294944 | tf_op jit(solution)/shard_map/all_to_all | solution.py:226
  563.1 3.4 gather_fusion.1
  571.7 11.7 %cholesky.103 = f32[128,128]{1,0:T(8,128)S(1)} custom-call(f32[128,128]{1,0:T(8,128)S(1)} %cholesky.263), custom_call_target="Cholesky" | custom-call | tf_op jit(solution)/shard_map/jit(cholesky)/cholesky | solution.py:149
  583.6 3.1 copy.159
  586.6 9.8 %custom-call.34 = f32[1,128,128]{1,2,0:T(8,128)S(1)} custom-call(f32[1,128,128]{2,1,0:T(8,128)S(1)} %get-tuple-element.463), custom_call_target="InvertDiagBlocksLowerTriangular" | custom-call | tf_op jit(solution)/shard_map/jit(cholesky)/cholesky | solution.py:149
  598.9 11.7 %cholesky.215 = f32[128,128]{1,0:T(8,128)S(1)} custom-call(f32[128,128]{1,0:T(8,128)S(1)} %cholesky.267), custom_call_target="Cholesky" | custom-call | tf_op jit(solution)/shard_map/jit(cholesky)/cholesky | solution.py:149
  612.0 9.8 %custom-call.35 = f32[1,128,128]{1,2,0:T(8,128)S(1)} custom-call(f32[1,128,128]{2,1,0:T(8,128)S(1)} %get-tuple-element.460), custom_call_target="InvertDiagBlocksLowerTriangular" | custom-call | tf_op jit(solution)/shard_map/jit(cholesky)/cholesky | solution.py:149
  623.4 11.9 %cholesky.236 = f32[128,128]{1,0:T(8,128)S(1)} custom-call(f32[128,128]{1,0:T(8,128)S(1)} %cholesky.272), custom_call_target="Cholesky" | custom-call | tf_op jit(solution)/shard_map/jit(cholesky)/cholesky | solution.py:149
  636.0 9.8 %custom-call.36 = f32[1,128,128]{1,2,0:T(8,128)S(1)} custom-call(f32[1,128,128]{2,1,0:T(8,128)S(1)} %get-tuple-element.457), custom_call_target="InvertDiagBlocksLowerTriangular" | custom-call | tf_op jit(solution)/shard_map/jit(cholesky)/cholesky | solution.py:149
  647.3 11.7 %cholesky.253 = f32[128,128]{1,0:T(8,128)S(1)} custom-call(f32[128,128]{1,0:T(8,128)S(1)} %convolution_subtract_fusion.2), custom_call_target="Cholesky" | custom-call | tf_op jit(solution)/shard_map/jit(cholesky)/cholesky | solution.py:149
  663.3 13.5 %while.36 = (s32[]{:T(128)}, f32[512,512]{1,0:T(8,128)}, s32[4,2]{0,1:T(2,128)S(1)}, f32[4,128,128]{2,1,0:T(8,128)}, s32[]{:T(128)}) while((s32[]{:T(128)}, f32[512,512]{1,0:T(8,128)}, s32[4,2]{0,1:T(2,128)S(1)}, f32[4,128,128]{2,1,0:T(8,128)}, s32[]{:T(128)}) %tuple.118), condition=%wide.while_cond, body=%wide.while_body.sunk | while | flops 2 | bytes 132705 | solution.py:151
  676.8 40.1 %custom-call.37 = f32[4,128,128]{1,2,0:T(8,128)S(1)} custom-call(f32[4,128,128]{2,1,0:T(8,128)} %get-tuple-element.247), custom_call_target="InvertDiagBlocksLowerTriangular" | custom-call | tf_op jit(solution)/shard_map/jit(_solve_triangular)/triangular_solve | solution.py:151
  717.0 3.7 gather_fusion.2
  729.6 14.9 %while.37 = (s32[]{:T(128)}, f32[16,9216]{1,0:T(8,128)S(1)}, f32[16,144]{1,0:T(8,128)S(1)}, f32[16,16,16]{2,1,0:T(8,128)S(1)}, f32[16,9216]{1,0:T(8,128)S(1)}, /*index=5*/s32[]{:T(128)}, s32[]{:T(128)}) while((s32[]{:T(128)}, f32[16,9216]{1,0:T(8,128)S(1)}, f32[16,144]{1,0:T(8,128)S(1)}, f32[16,16,16]{2,1,0:T(8,128)S(1)}, ...), condition=%wide.region_16.18_spmd.clone, body=%wide.region_15.17_spmd.clone.sunk | while | flops 28753924 | bytes 1921823 | solution.py:174
  (1584 shorter events, 350.7 us)
Async XLA Ops:
  0.0 1.2 copy-start
  4.8 419.7 %all-to-all-start = ((bf16[1,128,6,2,192]{1,3,2,0,4:T(2,128)(2,1)}), bf16[1,128,6,2,192]{1,3,2,0,4:T(2,128)(2,1)S(1)}, u32[]{:S(2)}, u32[]{:S(2)}) async-start(bf16[1,128,6,2,192]{1,3,2,0,4:T(2,128)(2,1)} %copy.123), calls=%async_computation | async-start | bytes 1179648 | tf_op jit(solution)/shard_map/all_to_all | solution.py:205
  424.5 2.5 copy-start.5
  424.5 1.3 copy-start.3
  424.5 1.7 copy-start.7
  427.0 14.3 %copy-start.14 = (f32[2,128]{1,0:T(2,128)S(1)}, f32[2,128]{1,0:T(2,128)}, u32[]{:S(2)}) copy-start(f32[2,128]{1,0:T(2,128)} %param.21) | copy-start | bytes 3076
  428.8 31.2 %all-to-all-start.1 = ((bf16[1,128,192,2,6]{1,3,4,0,2:T(2,128)(2,1)}), bf16[1,128,192,2,6]{1,3,4,0,2:T(2,128)(2,1)S(1)}, u32[]{:S(2)}, u32[]{:S(2)}) async-start(bf16[1,128,192,2,6]{1,3,4,0,2:T(2,128)(2,1)} %copy.132), calls=%async_computation.1 | async-start | bytes 1179648 | tf_op jit(solution)/shard_map/all_to_all | solution.py:208
  460.0 1.2 copy-start.15
  468.7 28.5 %copy-start.4 = (bf16[6,192,192,1]{2,0,1,3:T(8,128)(2,1)S(1)}, bf16[6,192,192,1]{2,0,1,3:T(8,128)(2,1)}, u32[]{:S(2)}) copy-start(bf16[6,192,192,1]{2,0,1,3:T(8,128)(2,1)} %get-tuple-element.452) | copy-start | bytes 1327108
  496.3 1.2 copy-start.8
  497.8 1.1 copy-start.6
  498.3 10.4 %copy-start.9 = (f32[1,1,16,144]{3,2,1,0:T(8,128)S(1)}, f32[1,1,16,144]{3,2,1,0:T(8,128)}, u32[]{:S(2)}) copy-start(f32[1,1,16,144]{3,2,1,0:T(8,128)} %param.29) | copy-start | bytes 27652
  498.3 10.5 %copy-start.10 = (s32[1,1,512]{2,1,0:T(1,128)S(1)}, s32[1,1,512]{2,1,0:T(1,128)}, u32[]{:S(2)}) copy-start(s32[1,1,512]{2,1,0:T(1,128)} %param.25) | copy-start | bytes 6148
  500.6 26.5 %all-to-all-start.3 = ((bf16[1,128,192,2,6]{1,3,4,0,2:T(2,128)(2,1)}), bf16[1,128,192,2,6]{1,3,4,0,2:T(2,128)(2,1)S(1)}, u32[]{:S(2)}, u32[]{:S(2)}) async-start(bf16[1,128,192,2,6]{1,3,4,0,2:T(2,128)(2,1)} %copy.147), calls=%async_computation.3 | async-start | bytes 1179648 | tf_op jit(solution)/shard_map/all_to_all | solution.py:208
  528.3 6.7 copy-start.2
  528.3 6.7 copy-start.11
  537.4 22.0 %all-to-all-start.4 = ((bf16[1,64,16,144]{3,1,0,2:T(8,128)(2,1)}), bf16[1,64,16,144]{3,1,0,2:T(8,128)(2,1)S(1)}, u32[]{:S(2)}, u32[]{:S(2)}) async-start(bf16[1,64,16,144]{3,1,0,2:T(8,128)(2,1)} %copy.153), calls=%async_computation.4 | async-start | bytes 1048576 | tf_op jit(solution)/shard_map/all_to_all | solution.py:226
  566.8 2.4 copy-start.12
  570.6 1.0 copy-start.1
  623.4 97.4 %copy-start.13 = (f32[1,1,512]{2,1,0:T(1,128)S(1)}, f32[1,1,512]{2,1,0:T(1,128)}, u32[]{:S(2)}) copy-start(f32[1,1,512]{2,1,0:T(1,128)} %param.27) | copy-start | bytes 6148
where the time goes:
time: 758 us; the launch traced here: 746 us
  other arithmetic  282 us (37%)
  local copies, waits for them, and re-layouts  162 us (21%)
  loops' own time  132 us (17%)
  matrix products  46.9 us (6%)
  waiting for transfers between devices  46.2 us (6%)
  starting transfers between devices  45.8 us (6%)
  blocking collectives  27 us (4%)
    dynamic_update_slice x192, other arithmetic, sphere_tables(): lax.scan(advance, (zero_rows, zero_rows), jnp.arange(degree_count, dtype=...  132 us
    another operation x1, loops' own time, sphere_tables(): lax.scan(advance, (zero_rows, zero_rows), jnp.arange(degree_count, dtype=...  131 us
    dynamic_slice x192, local copies, waits for them, and re-layouts, sphere_tables(): lax.scan(advance, (zero_rows, zero_rows), jnp.arange(degree_count, dtype=...  117 us
    another operation x15, other arithmetic, cholesky_solve(): factor = jnp.linalg.cholesky(system)  79.3 us
    another operation x3, other arithmetic, cholesky_solve(): jax.scipy.linalg.solve_triangular(factor, partial_solve, lower=True, tran...  41.3 us
    all_to_all x2, waiting for transfers between devices, shards(): lax.all_to_all(operand, 'sub', split_axis=2, concat_axis=4, tiled=True)  34.3 us
    all_to_all x1, blocking collectives, shards(): lax.all_to_all(operand, 'sub', split_axis=4, concat_axis=2, tiled=True)  27 us
    all_to_all x2, starting transfers between devices, shards(): lax.all_to_all(operand, 'sub', split_axis=2, concat_axis=4, tiled=True)  19.9 us
  transfers between devices with their start and end apart: 4, of which 3 were waited for; matrix products, arithmetic and copies ran while one was open for 37% of the time, Pallas kernels for 0%

commit v1 on v0

v1 whole, which is shorter than its diff:
```python
import functools
import math

import jax
import jax.numpy as jnp
import numpy as np
from jax import lax
from jax.experimental import pallas as pl
from jax.experimental.pallas import tpu as pltpu
from jax.sharding import PartitionSpec as P

F32 = jnp.float32
BF16 = jnp.bfloat16
EXACT = lax.Precision.HIGHEST
MESH = pl.DeviceIdType.MESH
NN = ((1,), (0,))
NT = ((1,), (1,))

LATS = 192
LONS = 384
DEGREES = 192
SUB = 32
GROUP = 16
BAND = 6
ROWS = 40
ALL = SUB * ROWS


def dot(a, b, dims, precision=None):
    return lax.dot_general(a, b, (dims, ((), ())), precision=precision, preferred_element_type=F32)


def dft_table():
    m = (BAND * np.arange(SUB)[None, :] + np.arange(BAND)[:, None]).reshape(-1)
    angle = 2.0 * np.pi * ((m[:, None] * np.arange(LONS)[None, :]) % LONS) / LONS
    return np.concatenate([np.cos(angle), -np.sin(angle)], axis=0)


def filter_tables():
    colatitude = (np.arange(LATS) + 0.5) * np.pi / LATS
    x, sine = np.cos(colatitude), np.sin(colatitude)
    m = np.arange(LATS, dtype=np.float64)[:, None]
    gammas = np.array([math.lgamma(v + 0.5) - math.lgamma(v + 1.0) for v in range(LATS)])[:, None]
    start = np.exp(
        0.5 * (np.log((2 * m + 1) / (4 * np.pi)) + gammas - 0.5 * np.log(np.pi)) + m * np.log(sine)[None, :]
    )
    earlier, previous, squares = np.zeros_like(start), np.zeros_like(start), np.zeros_like(start)
    for l in range(DEGREES + 1):
        up = np.sqrt((4.0 * l * l - 1.0) / np.maximum(l * l - m * m, 1.0)) if l else 0.0 * m
        low = np.sqrt(np.maximum((l - 1.0) ** 2 - m * m, 0.0) / max(4.0 * (l - 1.0) ** 2 - 1.0, 1.0))
        value = up * (x[None, :] * previous - low * earlier)
        value = np.where(l == m + 1, x[None, :] * np.sqrt(2 * m + 3) * start, value)
        value = np.where(l == m, start, np.where(l < m, 0.0, value))
        earlier, previous = previous, value
        if l < DEGREES:
            squares += value * value
    weight = 2.0 * np.pi * (np.pi / LATS) * sine[None, :] * np.where(m == 0, 1.0, 2.0) / LONS
    e = np.sqrt((DEGREES**2 - m * m) / (4.0 * DEGREES**2 - 1.0))
    per_order = [previous * e * weight, earlier * e * weight, squares * weight, previous, earlier]
    order = np.zeros((SUB, 8, SUB, ROWS), np.float32)
    place = np.zeros((8, SUB, ROWS), np.float32)
    place[2], place[3] = -1.0, -2.0
    for mm in range(BAND):
        for i in range(BAND):
            at = mm * BAND + i
            lats = BAND * np.arange(SUB) + i
            for k, table in enumerate(per_order):
                order[:, k, :, at] = table[BAND * np.arange(SUB) + mm][:, lats]
            high = x[lats].astype(np.float32)
            place[0, :, at], place[1, :, at] = high, x[lats] - high.astype(np.float64)
            place[2, :, at] = place[3, :, at] = mm
            place[4, :, at] = lats
    return order.reshape(SUB, 8, ALL), place.reshape(8, ALL)


def erf_gelu(x):
    return 0.5 * x * (1.0 + lax.erf(x * (1.0 / math.sqrt(2.0))))


def forecast_kernel(
    ic_ref, enc_ref, spec_ref, gain_ref, up_ref, down_ref, proj_ref, dft_ref, place_ref, order_hbm, out_ref,
    raw, member, filt, order, cols, gain, mix, spread, sent0, got0, sent1, got1, sent2, got2, sent3, got3,
    hidden, cast, tiles, send_sem, recv_sem, gsend_sem, grecv_sem, local_sem,
):
    me = lax.axis_index("sub")
    mine = lax.axis_index("group")

    def sub_peer(d):
        return lax.rem(me + d, SUB)

    def group_peer(d):
        return lax.rem(mine + d, GROUP)

    barrier = pltpu.get_barrier_semaphore()

    def greet_sub(d, _):
        pl.semaphore_signal(barrier, inc=1, device_id={"sub": sub_peer(d)}, device_id_type=MESH)
        return 0

    def greet_group(d, _):
        pl.semaphore_signal(barrier, inc=1, device_id={"group": group_peer(d)}, device_id_type=MESH)
        return 0

    lax.fori_loop(1, SUB, greet_sub, 0)
    lax.fori_loop(1, GROUP, greet_group, 0)
    fetch = pltpu.make_async_copy(order_hbm.at[me], order, local_sem.at[0])
    fetch.start()

    def exchange(stage, sent, got):
        def copy(d):
            return pltpu.make_async_remote_copy(
                src_ref=sent.at[sub_peer(d)], dst_ref=got.at[me], send_sem=send_sem.at[stage, d],
                recv_sem=recv_sem.at[stage, d], device_id={"sub": sub_peer(d)}, device_id_type=MESH)

        def start(d, _):
            copy(d).start()
            return 0

        def finish(d, _):
            copy(d).wait()
            return 0

        return (lambda: lax.fori_loop(1, SUB, start, 0)), (lambda: lax.fori_loop(1, SUB, finish, 0))

    def unpack(v, _):
        fields = ic_ref[v].astype(F32)
        for l in range(3):
            raw[l, pl.ds(pl.multiple_of(v * 8, 8), BAND), :] = fields[:, l * 128:(l + 1) * 128]
        return 0

    lax.fori_loop(0, 64, unpack, 0, unroll=4)
    spread[...] = jnp.zeros_like(spread)
    empty = jnp.zeros((64, LONS), BF16)

    def first_dft(i, _):
        fields = jnp.concatenate([raw[l, pl.ds(i, 64, stride=8), :] for l in range(3)], axis=1).astype(BF16)
        member[i] = fields
        real = jnp.concatenate([fields, empty], axis=0)
        imag = jnp.concatenate([empty, fields], axis=0)
        zonal = dot(dft_ref[0:192, :], real, NT) + dot(dft_ref[192:384, :], imag, NT)
        for mm in range(BAND):
            spread[0, pl.ds(mm * BAND + i, SUB, stride=ROWS), :] = zonal[mm * SUB:(mm + 1) * SUB, :]
        return 0

    lax.fori_loop(0, BAND, first_dft, 0)

    def stage_out(d, _):
        sent0[d] = spread[0, pl.ds(pl.multiple_of(d * ROWS, 8), ROWS), :].astype(BF16)
        return 0

    lax.fori_loop(0, SUB, stage_out, 0, unroll=4)
    pl.semaphore_wait(barrier, SUB + GROUP - 2)
    start, finish = exchange(0, sent0, got0)
    start()
    got0[me] = sent0[me]

    fetch.wait()
    cols[...] = jnp.concatenate([order[...], place_ref[...], jnp.zeros((112, ALL), F32)], axis=0).T

    def build(b, _):
        at = pl.ds(pl.multiple_of(b * 16, 16), 16)
        col = cols[at, :]
        top = col[:, 3:4] * order[1:2, :] - col[:, 4:5] * order[0:1, :]
        gap = (col[:, 8:9] - place_ref[0:1, :]) + (col[:, 9:10] - place_ref[1:2, :])
        same = col[:, 12:13] == place_ref[4:5, :]
        value = jnp.where(same, order[2:3, :], top / jnp.where(same, 1.0, gap))
        filt[at, :] = jnp.where(col[:, 11:12] == place_ref[2:3, :], value, 0.0).astype(BF16)
        return 0

    lax.fori_loop(0, ALL // 16, build, 0)
    gain[...] = jnp.concatenate([gain_ref[...], jnp.zeros((126, 128), F32)], axis=0).T
    enc = enc_ref[...]
    none = jnp.zeros((128, 64), BF16)
    enc_real = jnp.concatenate([enc, none], axis=1)
    enc_imag = jnp.concatenate([none, enc], axis=1)
    mix[0] = (dot(spec_ref[0, 0], enc_real, NN) - dot(spec_ref[0, 1], enc_imag, NN)).astype(BF16)
    mix[1] = (dot(spec_ref[0, 1], enc_real, NN) + dot(spec_ref[0, 0], enc_imag, NN)).astype(BF16)

    finish()

    def stage_in(got, part, dest):
        def body(d, _):
            block = got[d] if part is None else got[d, part]
            dest[pl.ds(pl.multiple_of(d * ROWS, 8), ROWS), :] = block.astype(F32)
            return 0
        lax.fori_loop(0, SUB, body, 0, unroll=4)

    stage_in(got0, None, spread.at[0])
    source = spread[0].astype(BF16)
    for b in range(4):
        filtered = dot(filt[b * 320:(b + 1) * 320, :], source, NN)
        for k in range(8):
            sent1[b * 8 + k] = filtered[k * ROWS:(k + 1) * ROWS, :].astype(BF16)
    start, finish = exchange(1, sent1, got1)
    start()
    got1[me] = sent1[me]
    finish()

    def latitude(i, part):
        return jnp.concatenate(
            [spread[part, pl.ds(mm * BAND + i, SUB, stride=ROWS), :] for mm in range(BAND)], axis=0).astype(BF16)

    def pointwise(layer, summed):
        centred = summed - jnp.mean(summed, axis=0, keepdims=True)
        spread_of = jnp.mean(centred * centred, axis=0, keepdims=True)
        normed = (centred * lax.rsqrt(spread_of + 1e-05) * gain[:, layer:layer + 1]).astype(BF16)
        lifted = erf_gelu(dot(up_ref[layer], normed, NN)).astype(BF16)
        return (summed + dot(down_ref[layer], lifted, NN)).astype(BF16)

    stage_in(got1, None, spread.at[0])

    def first_back(i, _):
        back = latitude(i, 0)
        real = dot(mix[0], back, NT).astype(BF16)
        imag = dot(mix[1], back, NT).astype(BF16)
        summed = dot(enc_ref[...], member[i], NN)
        summed = summed + dot(real, dft_ref[0:192, :], NN) + dot(imag, dft_ref[192:384, :], NN)
        hidden[i] = pointwise(0, summed)
        return 0

    lax.fori_loop(0, BAND, first_back, 0)

    def second_dft(i, _):
        zonal = dot(dft_ref[...], hidden[i], NT)
        for part in range(2):
            for mm in range(BAND):
                at = part * 192 + mm * SUB
                spread[part, pl.ds(mm * BAND + i, SUB, stride=ROWS), :] = zonal[at:at + SUB, :]
        return 0

    spread[...] = jnp.zeros_like(spread)
    lax.fori_loop(0, BAND, second_dft, 0)

    def stage_out2(d, _):
        for part in range(2):
            sent2[d, part] = spread[part, pl.ds(pl.multiple_of(d * ROWS, 8), ROWS), :].astype(BF16)
        return 0

    lax.fori_loop(0, SUB, stage_out2, 0, unroll=2)
    start, finish = exchange(2, sent2, got2)
    start()
    got2[me] = sent2[me]
    finish()
    stage_in(got2, 0, spread.at[0])
    stage_in(got2, 1, spread.at[1])
    source = jnp.concatenate([spread[0].astype(BF16), spread[1].astype(BF16)], axis=1)
    for b in range(4):
        filtered = dot(filt[b * 320:(b + 1) * 320, :], source, NN)
        for k in range(8):
            for part in range(2):
                sent3[b * 8 + k, part] = filtered[k * ROWS:(k + 1) * ROWS, part * 128:(part + 1) * 128].astype(BF16)
    start, finish = exchange(3, sent3, got3)
    start()
    got3[me] = sent3[me]
    finish()
    stage_in(got3, 0, spread.at[0])
    stage_in(got3, 1, spread.at[1])

    def second_back(i, _):
        back_real = latitude(i, 0)
        back_imag = latitude(i, 1)
        w_real, w_imag = spec_ref[1, 0], spec_ref[1, 1]
        real = (dot(w_real, back_real, NT) - dot(w_imag, back_imag, NT)).astype(BF16)
        imag = (dot(w_imag, back_real, NT) + dot(w_real, back_imag, NT)).astype(BF16)
        summed = hidden[i].astype(F32)
        summed = summed + dot(real, dft_ref[0:192, :], NN) + dot(imag, dft_ref[192:384, :], NN)
        fields = member[i].astype(F32) + dot(proj_ref[...], pointwise(1, summed), NN)
        for l in range(3):
            cast[3 * i + l] = fields[:, l * 128:(l + 1) * 128]
        return 0

    lax.fori_loop(0, BAND, second_back, 0)

    lane = lax.broadcasted_iota(jnp.int32, (8, 128), 1)

    def window(w, begin):
        first, turn = begin // 128, begin % 128
        def piece(j):
            return cast[min(max(j, 0), 17), pl.ds(w, 8, stride=8), :]
        if turn == 0:
            return piece(first)
        return jnp.where(
            lane < 128 - turn, pltpu.roll(piece(first), 128 - turn, 1), pltpu.roll(piece(first + 1), 128 - turn, 1))

    for g in range(GROUP):
        columns = []
        for t in range(9):
            value = window(t, 144 * g - 16 * t) if t < 8 else None
            if t > 0:
                before = window(t - 1, 144 * (g + 1) - 16 * t)
                value = before if value is None else jnp.where(lane < 16 * t, before, value)
            columns.append(value)
        tiles[g] = jnp.concatenate(columns, axis=0).astype(BF16)

    def tile_copy(d):
        return pltpu.make_async_remote_copy(
            src_ref=tiles.at[group_peer(d)], dst_ref=out_ref.at[mine], send_sem=gsend_sem.at[d],
            recv_sem=grecv_sem.at[d], device_id={"group": group_peer(d)}, device_id_type=MESH)

    def tile_start(d, _):
        tile_copy(d).start()
        return 0

    def tile_finish(d, _):
        tile_copy(d).wait()
        return 0

    own = pltpu.make_async_copy(tiles.at[mine], out_ref.at[mine], local_sem.at[1])
    own.start()
    lax.fori_loop(1, GROUP, tile_start, 0)
    own.wait()
    lax.fori_loop(1, GROUP, tile_finish, 0)


def forecast(ic, enc, spec, gain, up, down, proj):
    order, place = filter_tables()
    v = pl.BlockSpec(memory_space=pltpu.VMEM)
    block = (SUB, ROWS, 128)
    pair = (SUB, 2, ROWS, 128)
    return pl.pallas_call(
        forecast_kernel,
        out_shape=jax.ShapeDtypeStruct((GROUP, 72, 128), BF16),
        in_specs=[v] * 9 + [pl.BlockSpec(memory_space=pl.ANY)],
        out_specs=pl.BlockSpec(memory_space=pl.ANY),
        scratch_shapes=[
            pltpu.VMEM((3, 512, 128), F32),
            pltpu.VMEM((BAND, 64, LONS), BF16),
            pltpu.VMEM((ALL, ALL), BF16),
            pltpu.VMEM((8, ALL), F32),
            pltpu.VMEM((ALL, 128), F32),
            pltpu.VMEM((128, 128), F32),
            pltpu.VMEM((2, 128, 128), BF16),
            pltpu.VMEM((2, ALL, 128), F32),
            pltpu.VMEM(block, BF16), pltpu.VMEM(block, BF16), pltpu.VMEM(block, BF16), pltpu.VMEM(block, BF16),
            pltpu.VMEM(pair, BF16), pltpu.VMEM(pair, BF16), pltpu.VMEM(pair, BF16), pltpu.VMEM(pair, BF16),
            pltpu.VMEM((BAND, 128, LONS), BF16),
            pltpu.VMEM((18, 64, 128), F32),
            pltpu.VMEM((GROUP, 72, 128), BF16),
            pltpu.SemaphoreType.DMA((4, SUB)), pltpu.SemaphoreType.DMA((4, SUB)),
            pltpu.SemaphoreType.DMA((GROUP,)), pltpu.SemaphoreType.DMA((GROUP,)),
            pltpu.SemaphoreType.DMA((2,)),
        ],
        compiler_params=pltpu.CompilerParams(collective_id=0, has_side_effects=True, vmem_limit_bytes=48 << 20),
        name="forecast",
    )(ic, enc, spec, gain, up, down, proj, jnp.asarray(dft_table(), BF16), jnp.asarray(place), jnp.asarray(order))


def reduce_rows(pieces):
    rows = [[p[a:a + 1, :] for p in pieces] for a in range(8)]
    d = [[jnp.broadcast_to(rows[a][0][:, b:b + 1], (1, 128)) for b in range(8)] for a in range(8)]
    for a in range(8):
        inv = 1.0 / d[a][a]
        rows[a] = [x * inv for x in rows[a]]
        top = [None if b <= a else d[a][b] * inv for b in range(8)]
        d[a] = top
        for c in range(8):
            if c == a:
                continue
            f = d[c][a]
            rows[c] = [x - f * y for x, y in zip(rows[c], rows[a])]
            d[c] = [d[c][b] if b <= a else d[c][b] - f * top[b] for b in range(8)]
    return [jnp.concatenate([rows[a][l] for a in range(8)], axis=0) for l in range(len(pieces))]


def jordan(sys_ref, n, width):
    pieces = width // 128
    blocks = n // 8
    heads = n // 128
    def shift(vals, rows):
        lane = lax.broadcasted_iota(jnp.int32, (rows, 128), 1)
        r = [pltpu.roll(v, 120, 1) for v in vals[:heads]]
        if heads == 1:
            return r + list(vals[1:])
        return [jnp.where(lane < 120, r[h], r[(h + 1) % heads]) for h in range(heads)] + list(vals[heads:])
    def load(r):
        at = pl.ds(pl.multiple_of(r * 8, 8), 8)
        return [sys_ref[at, l * 128:(l + 1) * 128] for l in range(pieces)]
    def step(blk, red):
        nxt = lax.rem(blk + 1, blocks)
        x = load(nxt)
        c = [jnp.broadcast_to(x[0][:, b:b + 1], (8, 128)) for b in range(8)]
        for b in range(8):
            x = [v - c[b] * r[b:b + 1, :] for v, r in zip(x, red)]
        new = reduce_rows(shift(x, 8))
        left = sys_ref[:, 0:8]
        full = [sys_ref[:, l * 128:(l + 1) * 128] - dot(left, red[l], NN, EXACT) for l in range(pieces)]
        full = shift(full, n)
        for l in range(pieces):
            sys_ref[:, l * 128:(l + 1) * 128] = full[l]
        keep = shift(list(red), 8)
        at = pl.ds(pl.multiple_of(blk * 8, 8), 8)
        for l in range(pieces):
            sys_ref[at, l * 128:(l + 1) * 128] = keep[l]
        return tuple(new)
    lax.fori_loop(0, blocks, step, tuple(reduce_rows(load(0))))


def analysis_kernel(tile_ref, count_ref, pos_ref, val_ref, var_ref, mod_ref, out_ref, raw, state, pert, sysm, mtab):
    for q in range(16):
        raw[q * 72:(q + 1) * 72, :] = tile_ref[q].astype(F32)
    def collect(r, _):
        rows = raw[pl.ds(r, 16, stride=72), :]
        at = pl.ds(pl.multiple_of(r * 16, 16), 16)
        state[at, :] = rows
        mean = jnp.sum(rows, axis=0, keepdims=True) * (1.0 / 16)
        pert[at, :] = rows - mean
        return 0
    lax.fori_loop(0, 72, collect, 0, unroll=8)
    pos = pos_ref[...]
    col = pos >> 7
    lane = pos & 127
    u = jnp.floor((col.astype(F32) + 0.5) * (1.0 / 9)).astype(jnp.int32)
    row = (col - 9 * u) * 8 + u
    cell = pos - 144 * jnp.floor((pos.astype(F32) + 0.5) * (1.0 / 144)).astype(jnp.int32)
    pick = (lax.broadcasted_iota(jnp.int32, (128, 512), 0) == lane).astype(F32).astype(BF16)
    pick_cell = (lax.broadcasted_iota(jnp.int32, (144, 512), 0) == cell).astype(F32).astype(BF16)
    def gather(i, acc):
        at = pl.ds(pl.multiple_of(i * 128, 128), 128)
        part = dot(state[at, :].astype(BF16), pick, NN)
        for k in range(8):
            acc = acc + jnp.where(row == i * 8 + k, part[k * 16:(k + 1) * 16, :], 0.0)
        return acc
    picked = lax.fori_loop(0, 9, gather, jnp.zeros((16, 512), F32))
    mod = mod_ref[...]
    hi = mod.astype(BF16)
    rest = mod - hi.astype(F32)
    mid = rest.astype(BF16)
    low = (rest - mid.astype(F32)).astype(BF16)
    mod_at = dot(hi, pick_cell, NN) + dot(mid, pick_cell, NN) + dot(low, pick_cell, NN)
    valid = lax.broadcasted_iota(jnp.int32, (1, 512), 1) < count_ref[0, 0]
    root = jnp.where(valid, lax.rsqrt(var_ref[...]), 0.0)
    dev = (picked - jnp.sum(picked, axis=0, keepdims=True) * (1.0 / 16)) * (root * (1.0 / math.sqrt(15.0)))
    innov = jnp.where(valid, val_ref[...] - picked, 0.0) * root
    anom = jnp.concatenate([dev[k:k + 1, :] * mod_at for k in range(16)], axis=0)
    eye = (lax.broadcasted_iota(jnp.int32, (256, 256), 0) == lax.broadcasted_iota(jnp.int32, (256, 256), 1)).astype(F32)
    sysm[:, 0:256] = dot(anom, anom, NT, EXACT) + eye
    rhs = jnp.concatenate([innov, jnp.zeros((112, 512), F32)], axis=0)
    sysm[:, 256:384] = dot(anom, rhs, NT, EXACT)
    jordan(sysm, 256, 384)
    wt = sysm[:, 256:384].T[0:16, :]
    spread = jnp.concatenate([wt] * 16, axis=0)
    same = (lax.broadcasted_iota(jnp.int32, (256, 256), 0) // 16) == (lax.broadcasted_iota(jnp.int32, (256, 256), 1) // 16)
    spread = jnp.where(same, spread, 0.0)
    modk = jnp.concatenate([mod * (1.0 / math.sqrt(15.0))] * 16, axis=0)
    coef = dot(spread, modk, NN, EXACT)
    for t in range(9):
        start = (128 * t) % 144
        if start + 128 <= 144:
            part = coef[:, start:start + 128]
        else:
            part = jnp.concatenate([coef[:, start:144], coef[:, 0:start - 16]], axis=1)
        mtab[t] = part
    def apply(t, _):
        for u8 in range(8):
            at = pl.multiple_of((t * 8 + u8) * 16, 16)
            acc = state[pl.ds(at, 16), :]
            p = pert[pl.ds(at, 16), :]
            for k in range(16):
                acc = acc + mtab[t, k * 16:(k + 1) * 16, :] * p[k:k + 1, :]
            out_ref[:, pl.ds(pl.multiple_of((9 * u8 + t) * 128, 128), 128)] = acc.astype(BF16)
        return 0
    lax.fori_loop(0, 9, apply, 0)


def analysis(tile, count, pos, val, var, mod):
    v = pl.BlockSpec(memory_space=pltpu.VMEM)
    return pl.pallas_call(
        analysis_kernel,
        out_shape=jax.ShapeDtypeStruct((16, 9216), BF16),
        in_specs=[v, pl.BlockSpec(memory_space=pltpu.SMEM), v, v, v, v],
        out_specs=v,
        scratch_shapes=[pltpu.VMEM((1152, 128), F32), pltpu.VMEM((1152, 128), F32), pltpu.VMEM((1152, 128), F32),
                        pltpu.VMEM((256, 384), F32), pltpu.VMEM((9, 256, 128), F32)],
        compiler_params=pltpu.CompilerParams(vmem_limit_bytes=48 << 20),
        name="analysis",
    )(tile, count, pos, val, var, mod)


def shards(ic, enc, spec, gain, up, down, proj, pos, count, value, var, mod):
    tile = forecast(ic[0], enc, spec, gain, up, down, proj)
    out = analysis(tile, count, pos[0], value[0], var[0], mod[0, 0])
    return out[None, None]


def solution(mesh):
    part = P("sub", "group", None)
    return jax.shard_map(
        shards,
        mesh=mesh,
        in_specs=(P("group", None, "sub", None),) + (P(),) * 6
        + (part, P("sub", "group"), part, part, P("sub", "group", None, None)),
        out_specs=P("sub", "group", None, None),
        check_vma=False,
    )
```

time: 758 us -> 140 us (0.18); the launches traced: 746 us -> 140 us
  other arithmetic: 282 us -> 0 us
  local copies, waits for them, and re-layouts: 162 us -> 9.15 us
  loops' own time: 132 us -> 0 us
  Pallas kernels: 0 us -> 130 us
  matrix products: 46.9 us -> 0 us
  waiting for transfers between devices: 46.2 us -> 0 us
  starting transfers between devices: 45.8 us -> 0 us
  blocking collectives: 27 us -> 0 us
    another operation x3 -> x0, loops' own time: 132 us -> none  [the longest x1 131 us: sphere_tables(): lax.scan(advance, (zero_rows, zero_rows), jnp.arange(degree_count, dtype=...]
    dynamic_update_slice x192 -> x0, other arithmetic: 132 us -> none  [sphere_tables(): lax.scan(advance, (zero_rows, zero_rows), jnp.arange(degree_count, dtype=...]
    pallas_call x0 -> x2, Pallas kernels: none -> 130 us  [the longest x1 107 us: forecast(): pl.pallas_call(forecast_kernel, out_shape=jax.ShapeDtypeStruct((GROUP, 72...]
    another operation x21 -> x0, other arithmetic: 122 us -> none  [the longest x15 79.3 us: cholesky_solve(): factor = jnp.linalg.cholesky(system)]
    dynamic_slice x224 -> x0, local copies, waits for them, and re-layouts: 117 us -> none  [the longest x192 117 us: sphere_tables(): lax.scan(advance, (zero_rows, zero_rows), jnp.arange(degree_count, dtype=...]
    all_to_all x4 -> x0, waiting for transfers between devices: 46.2 us -> none  [the longest x2 34.3 us: shards(): lax.all_to_all(operand, 'sub', split_axis=2, concat_axis=4, tiled=True)]
    all_to_all x4 -> x0, starting transfers between devices: 45.8 us -> none  [the longest x2 19.9 us: shards(): lax.all_to_all(operand, 'sub', split_axis=2, concat_axis=4, tiled=True)]
    dot_general x34 -> x0, matrix products: 33.2 us -> none  [the longest x16 19.6 us: product(): jnp.einsum(pattern, first_operand, second_operand, preferred_element_type...]
  transfers between devices with their start and end apart: 4 -> 0, of which waited for: 3 -> 0; matrix products, arithmetic and copies ran while one was open for 37% -> 0% of each run, Pallas kernels for 0% -> 0%
where the time goes in v1:
time: 140 us
  Pallas kernels  130 us (93%)
  local copies, waits for them, and re-layouts  9.15 us (7%)
    pallas_call x1, Pallas kernels, forecast(): pl.pallas_call(forecast_kernel, out_shape=jax.ShapeDtypeStruct((GROUP, 72...  107 us
    pallas_call x1, Pallas kernels, analysis(): pl.pallas_call(analysis_kernel, out_shape=jax.ShapeDtypeStruct((16, 9216)...  22.5 us
    unnamed x26, local copies, waits for them, and re-layouts  9.15 us

profile of v1, /device:TPU:56, one launch (start us, length us, event | category | flops | bytes accessed | tf_op | source)
XLA Modules:
  0.0 139.6 jit_solution(13788514536621670274)
XLA Ops:
  0.0 1.1 copy.19
  1.1 0.8 copy.17.enc_ref
  2.0 0.0 copy-start
  2.0 1.3 copy-done
  3.3 0.0 copy-start.1
  3.3 1.0 copy-done.1
  4.3 0.0 copy-start.2
  4.3 0.9 copy-done.2
  5.2 0.0 copy-start.3
  5.2 0.9 copy-done.3
  6.1 0.0 copy-start.4
  6.1 0.9 copy-done.4
  7.0 0.0 copy-start.5
  7.0 0.8 copy-done.5
  7.8 0.0 copy-start.6
  7.8 0.7 copy-done.6
  8.5 0.0 copy-start.11
  8.5 0.7 copy-done.11
  9.2 107.2 %forecast.1.tile_ref = bf16[16,72,128]{2,1,0:T(8,128)(2,1)S(1)} custom-call(bf16[64,6,384]{2,1,0:T(8,128)(2,1)S(1)} %bitcast.8, bf16[128,64]{1,0:T(8,128)(2,1)S(1)} %copy.17.enc_ref, bf16[2,2,128,128]{3,2,1,0:T(8,128)(2,1)S(1)} %copy-done.2, f32[2,128]{1,0:T(2,128)S(1)} %copy-done.11, bf16[2,256,128]{2,1,0:T(8,128)(2,1)S(1)} %copy-done.3, ...), custom_call_target="tpu_custom_call" | custom-call | tf_op jit(solution)/shard_map/forecast/pallas_call | solution.py:320
  117.1 0.0 copy-done.7
  117.1 0.0 copy-done.8
  117.1 0.0 copy-done.9
  117.1 0.0 copy-done.10
  117.1 22.5 %analysis.1 = bf16[16,9216]{1,0:T(8,128)(2,1)} custom-call(bf16[16,72,128]{2,1,0:T(8,128)(2,1)S(1)} %forecast.1.tile_ref, s32[1,1]{1,0:T(1,128)S(6)} %copy.20.count_ref, s32[1,512]{1,0:T(1,128)S(1)} %bitcast.10, f32[1,512]{1,0:T(1,128)S(1)} %bitcast.11, f32[1,512]{1,0:T(1,128)S(1)} %bitcast.12, f32[16,144]{1,0:T(8,128)S(1)} %bitcast.9), custom_call_target="tpu_custom_call" | custom-call | tf_op jit(solution)/shard_map/analysis/pallas_call | solution.py:467
  (4 shorter events, 0.0 us)
Async XLA Ops:
  2.0 1.3 copy-start
  3.3 1.0 copy-start.1
  4.3 0.9 copy-start.2
  5.2 0.9 copy-start.3
  6.1 0.9 copy-start.4
  7.0 0.8 copy-start.5
  7.8 0.7 copy-start.6
  8.5 0.7 copy-start.11
  9.2 107.9 %copy-start.7 = (f32[1,1,16,144]{3,2,1,0:T(8,128)S(1)}, f32[1,1,16,144]{3,2,1,0:T(8,128)}, u32[]{:S(2)}) copy-start(f32[1,1,16,144]{3,2,1,0:T(8,128)} %param.26) | copy-start | bytes 27652
  9.2 107.9 %copy-start.8 = (s32[1,1,512]{2,1,0:T(1,128)S(1)}, s32[1,1,512]{2,1,0:T(1,128)}, u32[]{:S(2)}) copy-start(s32[1,1,512]{2,1,0:T(1,128)} %param.22) | copy-start | bytes 6148
  9.2 107.9 %copy-start.9 = (f32[1,1,512]{2,1,0:T(1,128)S(1)}, f32[1,1,512]{2,1,0:T(1,128)}, u32[]{:S(2)}) copy-start(f32[1,1,512]{2,1,0:T(1,128)} %param.24) | copy-start | bytes 6148
  9.2 107.9 %copy-start.10 = (f32[1,1,512]{2,1,0:T(1,128)S(1)}, f32[1,1,512]{2,1,0:T(1,128)}, u32[]{:S(2)}) copy-start(f32[1,1,512]{2,1,0:T(1,128)} %param.25) | copy-start | bytes 6148

commit v2 on v1

--- a/solution.py
+++ b/solution.py
@@ -22,7 +22,10 @@
 SUB = 32
 GROUP = 16
 BAND = 6
-ROWS = 40
+HALF = BAND // 2
+USED = HALF * BAND
+GAP = 24
+ROWS = 2 * GAP
 ALL = SUB * ROWS
 
 
@@ -57,20 +60,16 @@
     weight = 2.0 * np.pi * (np.pi / LATS) * sine[None, :] * np.where(m == 0, 1.0, 2.0) / LONS
     e = np.sqrt((DEGREES**2 - m * m) / (4.0 * DEGREES**2 - 1.0))
     per_order = [previous * e * weight, earlier * e * weight, squares * weight, previous, earlier]
-    order = np.zeros((SUB, 8, SUB, ROWS), np.float32)
-    place = np.zeros((8, SUB, ROWS), np.float32)
-    place[2], place[3] = -1.0, -2.0
-    for mm in range(BAND):
-        for i in range(BAND):
-            at = mm * BAND + i
-            lats = BAND * np.arange(SUB) + i
-            for k, table in enumerate(per_order):
-                order[:, k, :, at] = table[BAND * np.arange(SUB) + mm][:, lats]
-            high = x[lats].astype(np.float32)
-            place[0, :, at], place[1, :, at] = high, x[lats] - high.astype(np.float64)
-            place[2, :, at] = place[3, :, at] = mm
-            place[4, :, at] = lats
-    return order.reshape(SUB, 8, ALL), place.reshape(8, ALL)
+    order = np.zeros((SUB, BAND, 8, 256), np.float32)
+    place = np.zeros((8, 256), np.float32)
+    place[0] = 2.0 + np.arange(256)
+    lats = (BAND * np.arange(SUB)[None, :] + np.arange(BAND)[:, None]).reshape(-1)
+    for k, table in enumerate(per_order):
+        order[:, :, k, :LATS] = table.reshape(SUB, BAND, LATS)[:, :, lats]
+    place[0, :LATS] = x[lats].astype(np.float32)
+    place[1, :LATS] = x[lats] - x[lats].astype(np.float32).astype(np.float64)
+    place[2] = np.arange(256)
+    return order, place
 
 
 def erf_gelu(x):
@@ -78,127 +77,152 @@
 
 
 def forecast_kernel(
-    ic_ref, enc_ref, spec_ref, gain_ref, up_ref, down_ref, proj_ref, dft_ref, place_ref, order_hbm, out_ref,
-    raw, member, filt, order, cols, gain, mix, spread, sent0, got0, sent1, got1, sent2, got2, sent3, got3,
-    hidden, cast, tiles, send_sem, recv_sem, gsend_sem, grecv_sem, local_sem,
+    ic_hbm, enc_hbm, spec_hbm, gain_hbm, up_hbm, down_hbm, proj_hbm, dft_hbm, place_hbm, order_hbm, out_ref,
+    fields, enc_ref, spec_ref, gain_ref, up_ref, down_ref, proj_ref, dft_ref, place_ref, order_ref,
+    filt, gain, mix, spread, result, source, sent0, got0, sent1, got1, sent2, got2, sent3, got3,
+    hidden, cast, tiles, send_sem, recv_sem, tile_send, tile_recv, local_sem,
 ):
-    me = lax.axis_index("sub")
-    mine = lax.axis_index("group")
-
-    def sub_peer(d):
-        return lax.rem(me + d, SUB)
-
-    def group_peer(d):
-        return lax.rem(mine + d, GROUP)
+    group = lax.axis_index("group")
+    sub = lax.axis_index("sub")
 
     barrier = pltpu.get_barrier_semaphore()
 
-    def greet_sub(d, _):
-        pl.semaphore_signal(barrier, inc=1, device_id={"sub": sub_peer(d)}, device_id_type=MESH)
+    def greet_subs(d, _):
+        pl.semaphore_signal(barrier, inc=1, device_id=(group, (sub + d) % SUB), device_id_type=MESH)
         return 0
 
-    def greet_group(d, _):
-        pl.semaphore_signal(barrier, inc=1, device_id={"group": group_peer(d)}, device_id_type=MESH)
+    def greet_tiles(d, _):
+        pl.semaphore_signal(barrier, inc=1, device_id=((group + d) % GROUP, sub), device_id_type=MESH)
         return 0
 
-    lax.fori_loop(1, SUB, greet_sub, 0)
-    lax.fori_loop(1, GROUP, greet_group, 0)
-    fetch = pltpu.make_async_copy(order_hbm.at[me], order, local_sem.at[0])
-    fetch.start()
-
-    def exchange(stage, sent, got):
-        def copy(d):
+    lax.fori_loop(1, SUB, greet_subs, 0)
+    lax.fori_loop(1, GROUP, greet_tiles, 0)
+
+    loads = {}
+    for n, (name, src, dst) in enumerate((
+        ("fields", ic_hbm, fields), ("dft", dft_hbm, dft_ref), ("order", order_hbm.at[sub], order_ref),
+        ("place", place_hbm, place_ref), ("enc", enc_hbm, enc_ref), ("spec", spec_hbm, spec_ref),
+        ("gain", gain_hbm, gain_ref), ("up", up_hbm, up_ref), ("down", down_hbm, down_ref),
+        ("proj", proj_hbm, proj_ref),
+    )):
+        loads[name] = pltpu.make_async_copy(src, dst, local_sem.at[n])
+        loads[name].start()
+
+    class Exchange:
+        def __init__(self, stage, sent, got):
+            self.stage, self.sent, self.got = stage, sent, got
+
+        def copy(self, half, d):
+            band = (sub + d) % SUB
             return pltpu.make_async_remote_copy(
-                src_ref=sent.at[sub_peer(d)], dst_ref=got.at[me], send_sem=send_sem.at[stage, d],
-                recv_sem=recv_sem.at[stage, d], device_id={"sub": sub_peer(d)}, device_id_type=MESH)
-
-        def start(d, _):
-            copy(d).start()
+                src_ref=self.sent.at[band, half], dst_ref=self.got.at[sub, half],
+                send_sem=send_sem.at[self.stage * 2 + half, d], recv_sem=recv_sem.at[self.stage * 2 + half, d],
+                device_id=(group, band), device_id_type=MESH)
+
+        def start(self, half):
+            def body(d, _):
+                self.copy(half, d).start()
+                return 0
+
+            lax.fori_loop(1, SUB, body, 0)
+            self.got[sub, half] = self.sent[sub, half]
+
+        def finish(self, half):
+            def body(d, _):
+                self.copy(half, d).wait()
+                return 0
+
+            lax.fori_loop(1, SUB, body, 0)
+
+    def row_of(i, mm):
+        return (i // HALF) * GAP + (i % HALF) * BAND + mm
+
+    def put(dest, i, mm, rows):
+        dest[pl.ds(row_of(i, mm), SUB, stride=ROWS), :] = rows
+
+    def take(src, i, mm):
+        return src[pl.ds(row_of(i, mm), SUB, stride=ROWS), :]
+
+    def stage_out(src, sent, half, part):
+        def body(d, _):
+            block = src[pl.ds(pl.multiple_of(d * ROWS + half * GAP, 8), USED), :].astype(BF16)
+            if part is None:
+                sent[d, half] = block
+            else:
+                sent[d, half, part] = block
             return 0
-
-        def finish(d, _):
-            copy(d).wait()
+        lax.fori_loop(0, SUB, body, 0, unroll=8)
+
+    def stage_in(got, half, part, dest):
+        def body(d, _):
+            block = got[d, half] if part is None else got[d, half, part]
+            dest[pl.ds(pl.multiple_of(d * ROWS + half * GAP, 8), USED), :] = block.astype(F32)
             return 0
-
-        return (lambda: lax.fori_loop(1, SUB, start, 0)), (lambda: lax.fori_loop(1, SUB, finish, 0))
-
-    def unpack(v, _):
-        fields = ic_ref[v].astype(F32)
-        for l in range(3):
-            raw[l, pl.ds(pl.multiple_of(v * 8, 8), BAND), :] = fields[:, l * 128:(l + 1) * 128]
-        return 0
-
-    lax.fori_loop(0, 64, unpack, 0, unroll=4)
-    spread[...] = jnp.zeros_like(spread)
+        lax.fori_loop(0, SUB, body, 0, unroll=8)
+
+    halves = [range(0, HALF), range(HALF, BAND)]
+    first, second = Exchange(0, sent0, got0), Exchange(1, sent1, got1)
+    third, fourth = Exchange(2, sent2, got2), Exchange(3, sent3, got3)
     empty = jnp.zeros((64, LONS), BF16)
-
-    def first_dft(i, _):
-        fields = jnp.concatenate([raw[l, pl.ds(i, 64, stride=8), :] for l in range(3)], axis=1).astype(BF16)
-        member[i] = fields
-        real = jnp.concatenate([fields, empty], axis=0)
-        imag = jnp.concatenate([empty, fields], axis=0)
-        zonal = dot(dft_ref[0:192, :], real, NT) + dot(dft_ref[192:384, :], imag, NT)
-        for mm in range(BAND):
-            spread[0, pl.ds(mm * BAND + i, SUB, stride=ROWS), :] = zonal[mm * SUB:(mm + 1) * SUB, :]
-        return 0
-
-    lax.fori_loop(0, BAND, first_dft, 0)
-
-    def stage_out(d, _):
-        sent0[d] = spread[0, pl.ds(pl.multiple_of(d * ROWS, 8), ROWS), :].astype(BF16)
-        return 0
-
-    lax.fori_loop(0, SUB, stage_out, 0, unroll=4)
-    pl.semaphore_wait(barrier, SUB + GROUP - 2)
-    start, finish = exchange(0, sent0, got0)
-    start()
-    got0[me] = sent0[me]
-
-    fetch.wait()
-    cols[...] = jnp.concatenate([order[...], place_ref[...], jnp.zeros((112, ALL), F32)], axis=0).T
-
-    def build(b, _):
-        at = pl.ds(pl.multiple_of(b * 16, 16), 16)
-        col = cols[at, :]
-        top = col[:, 3:4] * order[1:2, :] - col[:, 4:5] * order[0:1, :]
-        gap = (col[:, 8:9] - place_ref[0:1, :]) + (col[:, 9:10] - place_ref[1:2, :])
-        same = col[:, 12:13] == place_ref[4:5, :]
-        value = jnp.where(same, order[2:3, :], top / jnp.where(same, 1.0, gap))
-        filt[at, :] = jnp.where(col[:, 11:12] == place_ref[2:3, :], value, 0.0).astype(BF16)
-        return 0
-
-    lax.fori_loop(0, ALL // 16, build, 0)
+    loads["fields"].wait()
+    loads["dft"].wait()
+    for half in range(2):
+        for i in halves[half]:
+            here = fields[i]
+            real = jnp.concatenate([here, empty], axis=0)
+            imag = jnp.concatenate([empty, here], axis=0)
+            zonal = dot(dft_ref[0:192, :], real, NT) + dot(dft_ref[192:384, :], imag, NT)
+            for mm in range(BAND):
+                put(spread.at[0], i, mm, zonal[mm * SUB:(mm + 1) * SUB, :])
+        stage_out(spread.at[0], sent0, half, None)
+        if half == 0:
+            pl.semaphore_wait(barrier, SUB + GROUP - 2)
+        first.start(half)
+
+    loads["order"].wait()
+    loads["place"].wait()
+    for mm in range(BAND):
+        rows = order_ref[mm]
+        col = jnp.concatenate([rows, place_ref[...], jnp.zeros((112, 256), F32)], axis=0).T[0:LATS, :]
+        for b in range(4):
+            c = col[b * 48:(b + 1) * 48, :]
+            top = c[:, 3:4] * rows[1:2, :] - c[:, 4:5] * rows[0:1, :]
+            gap = (c[:, 8:9] - place_ref[0:1, :]) + (c[:, 9:10] - place_ref[1:2, :])
+            same = c[:, 10:11] == place_ref[2:3, :]
+            value = jnp.where(same, rows[2:3, :], top / jnp.where(same, 1.0, gap))
+            filt[mm, b * 48:(b + 1) * 48, :] = value.astype(BF16)
+    for name in ("enc", "spec", "gain", "up", "down", "proj"):
+        loads[name].wait()
     gain[...] = jnp.concatenate([gain_ref[...], jnp.zeros((126, 128), F32)], axis=0).T
-    enc = enc_ref[...]
+    enc = enc_ref[...].T
     none = jnp.zeros((128, 64), BF16)
     enc_real = jnp.concatenate([enc, none], axis=1)
     enc_imag = jnp.concatenate([none, enc], axis=1)
     mix[0] = (dot(spec_ref[0, 0], enc_real, NN) - dot(spec_ref[0, 1], enc_imag, NN)).astype(BF16)
     mix[1] = (dot(spec_ref[0, 1], enc_real, NN) + dot(spec_ref[0, 0], enc_imag, NN)).astype(BF16)
 
-    finish()
-
-    def stage_in(got, part, dest):
-        def body(d, _):
-            block = got[d] if part is None else got[d, part]
-            dest[pl.ds(pl.multiple_of(d * ROWS, 8), ROWS), :] = block.astype(F32)
-            return 0
-        lax.fori_loop(0, SUB, body, 0, unroll=4)
-
-    stage_in(got0, None, spread.at[0])
-    source = spread[0].astype(BF16)
-    for b in range(4):
-        filtered = dot(filt[b * 320:(b + 1) * 320, :], source, NN)
-        for k in range(8):
-            sent1[b * 8 + k] = filtered[k * ROWS:(k + 1) * ROWS, :].astype(BF16)
-    start, finish = exchange(1, sent1, got1)
-    start()
-    got1[me] = sent1[me]
-    finish()
-
     def latitude(i, part):
-        return jnp.concatenate(
-            [spread[part, pl.ds(mm * BAND + i, SUB, stride=ROWS), :] for mm in range(BAND)], axis=0).astype(BF16)
+        return jnp.concatenate([take(spread.at[part], i, mm) for mm in range(BAND)], axis=0).astype(BF16)
+
+    def apply_filter(parts, sent, exchange):
+        for mm in range(BAND):
+            for part in range(parts):
+                source[mm, :, part * 128:(part + 1) * 128] = jnp.concatenate(
+                    [take(spread.at[part], i, mm) for i in range(BAND)], axis=0).astype(BF16)
+        for half in range(2):
+            for mm in range(BAND):
+                filtered = dot(filt[mm, half * 96:(half + 1) * 96, 0:LATS], source[mm, :, 0:parts * 128], NN)
+                for part in range(parts):
+                    for k, i in enumerate(halves[half]):
+                        put(result.at[part], i, mm, filtered[k * SUB:(k + 1) * SUB, part * 128:(part + 1) * 128])
+            for part in range(parts):
+                stage_out(result.at[part], sent, half, part if parts > 1 else None)
+            exchange.start(half)
+
+    for half in range(2):
+        first.finish(half)
+        stage_in(got0, half, None, spread.at[0])
+    apply_filter(1, sent1, second)
 
     def pointwise(layer, summed):
         centred = summed - jnp.mean(summed, axis=0, keepdims=True)
@@ -207,56 +231,33 @@
         lifted = erf_gelu(dot(up_ref[layer], normed, NN)).astype(BF16)
         return (summed + dot(down_ref[layer], lifted, NN)).astype(BF16)
 
-    stage_in(got1, None, spread.at[0])
-
-    def first_back(i, _):
-        back = latitude(i, 0)
-        real = dot(mix[0], back, NT).astype(BF16)
-        imag = dot(mix[1], back, NT).astype(BF16)
-        summed = dot(enc_ref[...], member[i], NN)
-        summed = summed + dot(real, dft_ref[0:192, :], NN) + dot(imag, dft_ref[192:384, :], NN)
-        hidden[i] = pointwise(0, summed)
-        return 0
-
-    lax.fori_loop(0, BAND, first_back, 0)
-
-    def second_dft(i, _):
-        zonal = dot(dft_ref[...], hidden[i], NT)
+    for half in range(2):
+        second.finish(half)
+        stage_in(got1, half, None, spread.at[0])
+        for i in halves[half]:
+            back = latitude(i, 0)
+            real = dot(mix[0], back, NT).astype(BF16)
+            imag = dot(mix[1], back, NT).astype(BF16)
+            summed = dot(enc, fields[i], NN)
+            summed = summed + dot(real, dft_ref[0:192, :], NN) + dot(imag, dft_ref[192:384, :], NN)
+            after = pointwise(0, summed)
+            hidden[i] = after
+            zonal = dot(dft_ref[...], after, NT)
+            for part in range(2):
+                for mm in range(BAND):
+                    at = part * 192 + mm * SUB
+                    put(result.at[part], i, mm, zonal[at:at + SUB, :])
         for part in range(2):
-            for mm in range(BAND):
-                at = part * 192 + mm * SUB
-                spread[part, pl.ds(mm * BAND + i, SUB, stride=ROWS), :] = zonal[at:at + SUB, :]
-        return 0
-
-    spread[...] = jnp.zeros_like(spread)
-    lax.fori_loop(0, BAND, second_dft, 0)
-
-    def stage_out2(d, _):
+            stage_out(result.at[part], sent2, half, part)
+        third.start(half)
+
+    for half in range(2):
+        third.finish(half)
         for part in range(2):
-            sent2[d, part] = spread[part, pl.ds(pl.multiple_of(d * ROWS, 8), ROWS), :].astype(BF16)
-        return 0
-
-    lax.fori_loop(0, SUB, stage_out2, 0, unroll=2)
-    start, finish = exchange(2, sent2, got2)
-    start()
-    got2[me] = sent2[me]
-    finish()
-    stage_in(got2, 0, spread.at[0])
-    stage_in(got2, 1, spread.at[1])
-    source = jnp.concatenate([spread[0].astype(BF16), spread[1].astype(BF16)], axis=1)
-    for b in range(4):
-        filtered = dot(filt[b * 320:(b + 1) * 320, :], source, NN)
-        for k in range(8):
-            for part in range(2):
-                sent3[b * 8 + k, part] = filtered[k * ROWS:(k + 1) * ROWS, part * 128:(part + 1) * 128].astype(BF16)
-    start, finish = exchange(3, sent3, got3)
-    start()
-    got3[me] = sent3[me]
-    finish()
-    stage_in(got3, 0, spread.at[0])
-    stage_in(got3, 1, spread.at[1])
-
-    def second_back(i, _):
+            stage_in(got2, half, part, spread.at[part])
+    apply_filter(2, sent3, fourth)
+
+    def second_back(i):
         back_real = latitude(i, 0)
         back_imag = latitude(i, 1)
         w_real, w_imag = spec_ref[1, 0], spec_ref[1, 1]
@@ -264,12 +265,9 @@
         imag = (dot(w_imag, back_real, NT) + dot(w_real, back_imag, NT)).astype(BF16)
         summed = hidden[i].astype(F32)
         summed = summed + dot(real, dft_ref[0:192, :], NN) + dot(imag, dft_ref[192:384, :], NN)
-        fields = member[i].astype(F32) + dot(proj_ref[...], pointwise(1, summed), NN)
+        ahead = fields[i].astype(F32) + dot(proj_ref[...], pointwise(1, summed), NN)
         for l in range(3):
-            cast[3 * i + l] = fields[:, l * 128:(l + 1) * 128]
-        return 0
-
-    lax.fori_loop(0, BAND, second_back, 0)
+            cast[3 * i + l] = ahead[:, l * 128:(l + 1) * 128]
 
     lane = lax.broadcasted_iota(jnp.int32, (8, 128), 1)
 
@@ -282,7 +280,7 @@
         return jnp.where(
             lane < 128 - turn, pltpu.roll(piece(first), 128 - turn, 1), pltpu.roll(piece(first + 1), 128 - turn, 1))
 
-    for g in range(GROUP):
+    def slice_tile(g):
         columns = []
         for t in range(9):
             value = window(t, 144 * g - 16 * t) if t < 8 else None
@@ -292,57 +290,76 @@
             columns.append(value)
         tiles[g] = jnp.concatenate(columns, axis=0).astype(BF16)
 
-    def tile_copy(d):
+    def tile_copy(to, origin):
         return pltpu.make_async_remote_copy(
-            src_ref=tiles.at[group_peer(d)], dst_ref=out_ref.at[mine], send_sem=gsend_sem.at[d],
-            recv_sem=grecv_sem.at[d], device_id={"group": group_peer(d)}, device_id_type=MESH)
-
-    def tile_start(d, _):
-        tile_copy(d).start()
+            src_ref=tiles.at[to], dst_ref=out_ref.at[origin], send_sem=tile_send.at[to],
+            recv_sem=tile_recv.at[origin], device_id=(to, sub), device_id_type=MESH)
+
+    for half in range(2):
+        fourth.finish(half)
+        for part in range(2):
+            stage_in(got3, half, part, spread.at[part])
+        for i in halves[half]:
+            second_back(i)
+        for g in range(half * 8, half * 8 + 8):
+            slice_tile(g)
+
+        def tile_start(d, _):
+            to = half * 8 + (group + d) % 8
+
+            @pl.when(to != group)
+            def _():
+                tile_copy(to, group).start()
+
+            return 0
+
+        lax.fori_loop(0, 8, tile_start, 0)
+
+    def tile_finish(d, _):
+        other = (group + d) % GROUP
+        tile_copy(other, group).wait_send()
+        tile_copy(other, other).wait_recv()
         return 0
 
-    def tile_finish(d, _):
-        tile_copy(d).wait()
-        return 0
-
-    own = pltpu.make_async_copy(tiles.at[mine], out_ref.at[mine], local_sem.at[1])
+    own = pltpu.make_async_copy(tiles.at[group], out_ref.at[group], local_sem.at[10])
     own.start()
-    lax.fori_loop(1, GROUP, tile_start, 0)
     own.wait()
     lax.fori_loop(1, GROUP, tile_finish, 0)
 
 
 def forecast(ic, enc, spec, gain, up, down, proj):
     order, place = filter_tables()
-    v = pl.BlockSpec(memory_space=pltpu.VMEM)
-    block = (SUB, ROWS, 128)
-    pair = (SUB, 2, ROWS, 128)
+    hbm = pl.BlockSpec(memory_space=pltpu.HBM)
+    block = (SUB, 2, USED, 128)
+    pair = (SUB, 2, 2, USED, 128)
     return pl.pallas_call(
         forecast_kernel,
         out_shape=jax.ShapeDtypeStruct((GROUP, 72, 128), BF16),
-        in_specs=[v] * 9 + [pl.BlockSpec(memory_space=pl.ANY)],
+        in_specs=[hbm] * 10,
         out_specs=pl.BlockSpec(memory_space=pl.ANY),
         scratch_shapes=[
-            pltpu.VMEM((3, 512, 128), F32),
-            pltpu.VMEM((BAND, 64, LONS), BF16),
-            pltpu.VMEM((ALL, ALL), BF16),
-            pltpu.VMEM((8, ALL), F32),
-            pltpu.VMEM((ALL, 128), F32),
+            pltpu.VMEM((BAND, 64, LONS), BF16), pltpu.VMEM((64, 128), BF16), pltpu.VMEM((2, 2, 128, 128), BF16),
+            pltpu.VMEM((2, 128), F32), pltpu.VMEM((2, 256, 128), BF16), pltpu.VMEM((2, 128, 256), BF16),
+            pltpu.VMEM((64, 128), BF16), pltpu.VMEM((384, LONS), BF16), pltpu.VMEM((8, 256), F32),
+            pltpu.VMEM((BAND, 8, 256), F32),
+            pltpu.VMEM((BAND, LATS, 256), BF16),
             pltpu.VMEM((128, 128), F32),
             pltpu.VMEM((2, 128, 128), BF16),
             pltpu.VMEM((2, ALL, 128), F32),
+            pltpu.VMEM((2, ALL, 128), F32),
+            pltpu.VMEM((BAND, LATS, 256), BF16),
             pltpu.VMEM(block, BF16), pltpu.VMEM(block, BF16), pltpu.VMEM(block, BF16), pltpu.VMEM(block, BF16),
             pltpu.VMEM(pair, BF16), pltpu.VMEM(pair, BF16), pltpu.VMEM(pair, BF16), pltpu.VMEM(pair, BF16),
             pltpu.VMEM((BAND, 128, LONS), BF16),
             pltpu.VMEM((18, 64, 128), F32),
             pltpu.VMEM((GROUP, 72, 128), BF16),
-            pltpu.SemaphoreType.DMA((4, SUB)), pltpu.SemaphoreType.DMA((4, SUB)),
+            pltpu.SemaphoreType.DMA((8, SUB)), pltpu.SemaphoreType.DMA((8, SUB)),
             pltpu.SemaphoreType.DMA((GROUP,)), pltpu.SemaphoreType.DMA((GROUP,)),
-            pltpu.SemaphoreType.DMA((2,)),
+            pltpu.SemaphoreType.DMA((11,)),
         ],
-        compiler_params=pltpu.CompilerParams(collective_id=0, has_side_effects=True, vmem_limit_bytes=48 << 20),
+        compiler_params=pltpu.CompilerParams(collective_id=0, has_side_effects=True, vmem_limit_bytes=62 << 20),
         name="forecast",
-    )(ic, enc, spec, gain, up, down, proj, jnp.asarray(dft_table(), BF16), jnp.asarray(place), jnp.asarray(order))
+    )(jnp.transpose(ic, (1, 0, 2)), enc.T, spec, gain, up, down, proj, jnp.asarray(dft_table(), BF16), jnp.asarray(place), jnp.asarray(order))
 
 
 def reduce_rows(pieces):

time: 140 us -> 130 us (0.929)
  local copies, waits for them, and re-layouts: 9.15 us -> 0.97 us
  Pallas kernels: 130 us -> 128 us
    unnamed x26 -> x10, local copies, waits for them, and re-layouts: 9.15 us -> 0.97 us
    pallas_call x1, Pallas kernels: 107 us -> 105 us  [forecast(): pl.pallas_call(forecast_kernel, out_shape=jax.ShapeDtypeStruct((GROUP, 72...]
where the time goes in v2:
time: 130 us; the launch traced here: 129 us
  Pallas kernels  128 us (98%)
    pallas_call x1, Pallas kernels, forecast(): pl.pallas_call(forecast_kernel, out_shape=jax.ShapeDtypeStruct((GROUP, 72...  105 us
    pallas_call x1, Pallas kernels, analysis(): pl.pallas_call(analysis_kernel, out_shape=jax.ShapeDtypeStruct((16, 9216)...  22.8 us

profile of v2, /device:TPU:56, one launch (start us, length us, event | category | flops | bytes accessed | tf_op | source)
XLA Modules:
  0.0 129.4 jit_solution(11538846838805612920)
XLA Ops:
  0.0 0.0 copy-start.1
  0.0 0.0 copy-start.4
  0.0 0.0 copy-start.3
  0.0 0.0 copy-start.2
  0.7 104.9 %forecast.1.tile_ref = bf16[16,72,128]{2,1,0:T(8,128)(2,1)} custom-call(bf16[6,64,384]{2,1,0:T(8,128)(2,1)} %bitcast.13, bf16[64,128]{1,0:T(8,128)(2,1)} %bitcast.14, bf16[2,2,128,128]{3,2,1,0:T(8,128)(2,1)} %spec_hbm.1, f32[2,128]{1,0:T(2,128)} %gain_hbm.1, bf16[2,256,128]{2,1,0:T(8,128)(2,1)} %up_hbm.1, bf16[2,128,256]{2,1,0:T(8,128)(2,1)} %down_hbm.1, ...), custom_call_target="tpu_custom_call" | custom-call | tf_op jit(solution)/shard_map/forecast/pallas_call | solution.py:335
  105.6 0.0 copy-done.1
  105.6 0.0 copy-done.4
  105.6 0.0 copy-done.3
  105.7 0.0 copy-done.2
  105.7 0.0 copy-start
  105.7 1.0 copy-done
  106.6 22.8 %analysis.1 = bf16[16,9216]{1,0:T(8,128)(2,1)} custom-call(bf16[16,72,128]{2,1,0:T(8,128)(2,1)S(1)} %copy-done, s32[1,1]{1,0:T(1,128)S(6)} %copy.16.count_ref, s32[1,512]{1,0:T(1,128)S(1)} %bitcast.10, f32[1,512]{1,0:T(1,128)S(1)} %bitcast.11, f32[1,512]{1,0:T(1,128)S(1)} %bitcast.12, f32[16,144]{1,0:T(8,128)S(1)} %bitcast.9), custom_call_target="tpu_custom_call" | custom-call | tf_op jit(solution)/shard_map/analysis/pallas_call | solution.py:484
Async XLA Ops:
  0.0 105.6 %copy-start.1 = (f32[1,1,16,144]{3,2,1,0:T(8,128)S(1)}, f32[1,1,16,144]{3,2,1,0:T(8,128)}, u32[]{:S(2)}) copy-start(f32[1,1,16,144]{3,2,1,0:T(8,128)} %param.26) | copy-start | bytes 27652
  0.0 105.6 %copy-start.4 = (f32[1,1,512]{2,1,0:T(1,128)S(1)}, f32[1,1,512]{2,1,0:T(1,128)}, u32[]{:S(2)}) copy-start(f32[1,1,512]{2,1,0:T(1,128)} %param.25) | copy-start | bytes 6148
  0.0 105.6 %copy-start.3 = (f32[1,1,512]{2,1,0:T(1,128)S(1)}, f32[1,1,512]{2,1,0:T(1,128)}, u32[]{:S(2)}) copy-start(f32[1,1,512]{2,1,0:T(1,128)} %param.24) | copy-start | bytes 6148
  0.0 105.6 %copy-start.2 = (s32[1,1,512]{2,1,0:T(1,128)S(1)}, s32[1,1,512]{2,1,0:T(1,128)}, u32[]{:S(2)}) copy-start(s32[1,1,512]{2,1,0:T(1,128)} %param.22) | copy-start | bytes 6148
  105.7 1.0 copy-start

commit v3 on v2

--- a/solution.py
+++ b/solution.py
@@ -108,12 +108,17 @@
         loads[name] = pltpu.make_async_copy(src, dst, local_sem.at[n])
         loads[name].start()
 
+    def far_first(e):
+        k = (e // 2) % 8
+        z = (sub // 4 + 4 + (k // 2) * (1 - 2 * (k % 2)) - k % 2) % 8
+        return z * 4 + (sub // 2 + 1 - e // 16) % 2 * 2 + (sub + 1 + e) % 2
+
     class Exchange:
         def __init__(self, stage, sent, got):
             self.stage, self.sent, self.got = stage, sent, got
 
         def copy(self, half, d):
-            band = (sub + d) % SUB
+            band = far_first(d)
             return pltpu.make_async_remote_copy(
                 src_ref=self.sent.at[band, half], dst_ref=self.got.at[sub, half],
                 send_sem=send_sem.at[self.stage * 2 + half, d], recv_sem=recv_sem.at[self.stage * 2 + half, d],
@@ -124,7 +129,7 @@
                 self.copy(half, d).start()
                 return 0
 
-            lax.fori_loop(1, SUB, body, 0)
+            lax.fori_loop(0, SUB - 1, body, 0)
             self.got[sub, half] = self.sent[sub, half]
 
         def finish(self, half):
@@ -132,7 +137,7 @@
                 self.copy(half, d).wait()
                 return 0
 
-            lax.fori_loop(1, SUB, body, 0)
+            lax.fori_loop(0, SUB - 1, body, 0)
 
     def row_of(i, mm):
         return (i // HALF) * GAP + (i % HALF) * BAND + mm
@@ -362,54 +367,61 @@
     )(jnp.transpose(ic, (1, 0, 2)), enc.T, spec, gain, up, down, proj, jnp.asarray(dft_table(), BF16), jnp.asarray(place), jnp.asarray(order))
 
 
-def reduce_rows(pieces):
-    rows = [[p[a:a + 1, :] for p in pieces] for a in range(8)]
-    d = [[jnp.broadcast_to(rows[a][0][:, b:b + 1], (1, 128)) for b in range(8)] for a in range(8)]
+def reduce_rows(rows, at):
+    lines = [rows[a:a + 1, :] for a in range(8)]
+    d = [[jnp.broadcast_to(lines[a][:, at + b:at + b + 1], (1, 128)) for b in range(8)] for a in range(8)]
     for a in range(8):
         inv = 1.0 / d[a][a]
-        rows[a] = [x * inv for x in rows[a]]
+        lines[a] = lines[a] * inv
         top = [None if b <= a else d[a][b] * inv for b in range(8)]
         d[a] = top
         for c in range(8):
             if c == a:
                 continue
             f = d[c][a]
-            rows[c] = [x - f * y for x, y in zip(rows[c], rows[a])]
+            lines[c] = lines[c] - f * lines[a]
             d[c] = [d[c][b] if b <= a else d[c][b] - f * top[b] for b in range(8)]
-    return [jnp.concatenate([rows[a][l] for a in range(8)], axis=0) for l in range(len(pieces))]
-
-
-def jordan(sys_ref, n, width):
-    pieces = width // 128
-    blocks = n // 8
-    heads = n // 128
-    def shift(vals, rows):
+    return lines
+
+
+def inverse(block):
+    lane = lax.broadcasted_iota(jnp.int32, (64, 128), 1)
+    row = lax.broadcasted_iota(jnp.int32, (64, 128), 0)
+    both = jnp.where(lane < 64, block, (lane - 64 == row).astype(F32))
+    parts = [both[r * 8:(r + 1) * 8, :] for r in range(8)]
+    for step in range(8):
+        at = step * 8
+        lines = reduce_rows(parts[step], at)
+        for r in range(8):
+            if r == step:
+                continue
+            x = parts[r]
+            c = [jnp.broadcast_to(x[:, at + b:at + b + 1], (8, 128)) for b in range(8)]
+            terms = [c[b] * lines[b] for b in range(8)]
+            parts[r] = x - (((terms[0] + terms[1]) + (terms[2] + terms[3]))
+                            + ((terms[4] + terms[5]) + (terms[6] + terms[7])))
+        parts[step] = jnp.concatenate(lines, axis=0)
+    return jnp.concatenate(parts, axis=0)[:, 64:128]
+
+
+def jordan(sys_ref):
+    def shifted(left, right, rows):
         lane = lax.broadcasted_iota(jnp.int32, (rows, 128), 1)
-        r = [pltpu.roll(v, 120, 1) for v in vals[:heads]]
-        if heads == 1:
-            return r + list(vals[1:])
-        return [jnp.where(lane < 120, r[h], r[(h + 1) % heads]) for h in range(heads)] + list(vals[heads:])
-    def load(r):
-        at = pl.ds(pl.multiple_of(r * 8, 8), 8)
-        return [sys_ref[at, l * 128:(l + 1) * 128] for l in range(pieces)]
-    def step(blk, red):
-        nxt = lax.rem(blk + 1, blocks)
-        x = load(nxt)
-        c = [jnp.broadcast_to(x[0][:, b:b + 1], (8, 128)) for b in range(8)]
-        for b in range(8):
-            x = [v - c[b] * r[b:b + 1, :] for v, r in zip(x, red)]
-        new = reduce_rows(shift(x, 8))
-        left = sys_ref[:, 0:8]
-        full = [sys_ref[:, l * 128:(l + 1) * 128] - dot(left, red[l], NN, EXACT) for l in range(pieces)]
-        full = shift(full, n)
-        for l in range(pieces):
-            sys_ref[:, l * 128:(l + 1) * 128] = full[l]
-        keep = shift(list(red), 8)
-        at = pl.ds(pl.multiple_of(blk * 8, 8), 8)
-        for l in range(pieces):
-            sys_ref[at, l * 128:(l + 1) * 128] = keep[l]
-        return tuple(new)
-    lax.fori_loop(0, blocks, step, tuple(reduce_rows(load(0))))
+        left, right = pltpu.roll(left, 64, 1), pltpu.roll(right, 64, 1)
+        return jnp.where(lane < 64, left, right), jnp.where(lane < 64, right, left)
+
+    def step(blk, _):
+        at = pl.ds(pl.multiple_of(blk * 64, 64), 64)
+        inv = inverse(sys_ref[at, 0:128])
+        rows = dot(inv, sys_ref[at, :], NN, EXACT)
+        full = sys_ref[...] - dot(sys_ref[:, 0:64], rows, NN, EXACT)
+        sys_ref[:, 256:384] = full[:, 256:384]
+        sys_ref[:, 0:128], sys_ref[:, 128:256] = shifted(full[:, 0:128], full[:, 128:256], 256)
+        sys_ref[at, 256:384] = rows[:, 256:384]
+        sys_ref[at, 0:128], sys_ref[at, 128:256] = shifted(rows[:, 0:128], rows[:, 128:256], 64)
+        return 0
+
+    lax.fori_loop(0, 4, step, 0)
 
 
 def analysis_kernel(tile_ref, count_ref, pos_ref, val_ref, var_ref, mod_ref, out_ref, raw, state, pert, sysm, mtab):
@@ -453,7 +465,7 @@
     sysm[:, 0:256] = dot(anom, anom, NT, EXACT) + eye
     rhs = jnp.concatenate([innov, jnp.zeros((112, 512), F32)], axis=0)
     sysm[:, 256:384] = dot(anom, rhs, NT, EXACT)
-    jordan(sysm, 256, 384)
+    jordan(sysm)
     wt = sysm[:, 256:384].T[0:16, :]
     spread = jnp.concatenate([wt] * 16, axis=0)
     same = (lax.broadcasted_iota(jnp.int32, (256, 256), 0) // 16) == (lax.broadcasted_iota(jnp.int32, (256, 256), 1) // 16)

time: 130 us -> 121 us (0.931)
  Pallas kernels: 128 us -> 118 us
    pallas_call x1, Pallas kernels: 105 us -> 99.2 us  [forecast(): pl.pallas_call(forecast_kernel, out_shape=jax.ShapeDtypeStruct((GROUP, 72...]
    pallas_call x1, Pallas kernels: 22.8 us -> 18.7 us  [analysis(): pl.pallas_call(analysis_kernel, out_shape=jax.ShapeDtypeStruct((16, 9216)...]
where the time goes in v3:
time: 121 us; the launch traced here: 120 us
  Pallas kernels  118 us (98%)
    pallas_call x1, Pallas kernels, forecast(): pl.pallas_call(forecast_kernel, out_shape=jax.ShapeDtypeStruct((GROUP, 72...  99.2 us
    pallas_call x1, Pallas kernels, analysis(): pl.pallas_call(analysis_kernel, out_shape=jax.ShapeDtypeStruct((16, 9216)...  18.7 us

profile of v3, /device:TPU:56, one launch (start us, length us, event | category | flops | bytes accessed | tf_op | source)
XLA Modules:
  0.0 119.6 jit_solution(12995343009282463533)
XLA Ops:
  0.0 0.0 copy-start.1
  0.0 0.0 copy-start.4
  0.0 0.0 copy-start.3
  0.0 0.0 copy-start.2
  0.7 99.2 %forecast.1.tile_ref = bf16[16,72,128]{2,1,0:T(8,128)(2,1)} custom-call(bf16[6,64,384]{2,1,0:T(8,128)(2,1)} %bitcast.13, bf16[64,128]{1,0:T(8,128)(2,1)} %bitcast.14, bf16[2,2,128,128]{3,2,1,0:T(8,128)(2,1)} %spec_hbm.1, f32[2,128]{1,0:T(2,128)} %gain_hbm.1, bf16[2,256,128]{2,1,0:T(8,128)(2,1)} %up_hbm.1, bf16[2,128,256]{2,1,0:T(8,128)(2,1)} %down_hbm.1, ...), custom_call_target="tpu_custom_call" | custom-call | tf_op jit(solution)/shard_map/forecast/pallas_call | solution.py:340
  99.9 0.0 copy-done.1
  99.9 0.0 copy-done.4
  100.0 0.0 copy-done.3
  100.0 0.0 copy-done.2
  100.0 0.0 copy-start
  100.0 1.0 copy-done
  100.9 18.7 %analysis.1 = bf16[16,9216]{1,0:T(8,128)(2,1)} custom-call(bf16[16,72,128]{2,1,0:T(8,128)(2,1)S(1)} %copy-done, s32[1,1]{1,0:T(1,128)S(6)} %copy.16.count_ref, s32[1,512]{1,0:T(1,128)S(1)} %bitcast.10, f32[1,512]{1,0:T(1,128)S(1)} %bitcast.11, f32[1,512]{1,0:T(1,128)S(1)} %bitcast.12, f32[16,144]{1,0:T(8,128)S(1)} %bitcast.9), custom_call_target="tpu_custom_call" | custom-call | tf_op jit(solution)/shard_map/analysis/pallas_call | solution.py:496
Async XLA Ops:
  0.0 99.9 %copy-start.1 = (f32[1,1,16,144]{3,2,1,0:T(8,128)S(1)}, f32[1,1,16,144]{3,2,1,0:T(8,128)}, u32[]{:S(2)}) copy-start(f32[1,1,16,144]{3,2,1,0:T(8,128)} %param.26) | copy-start | bytes 27652
  0.0 99.9 %copy-start.4 = (f32[1,1,512]{2,1,0:T(1,128)S(1)}, f32[1,1,512]{2,1,0:T(1,128)}, u32[]{:S(2)}) copy-start(f32[1,1,512]{2,1,0:T(1,128)} %param.25) | copy-start | bytes 6148
  0.0 100.0 %copy-start.3 = (f32[1,1,512]{2,1,0:T(1,128)S(1)}, f32[1,1,512]{2,1,0:T(1,128)}, u32[]{:S(2)}) copy-start(f32[1,1,512]{2,1,0:T(1,128)} %param.24) | copy-start | bytes 6148
  0.0 100.0 %copy-start.2 = (s32[1,1,512]{2,1,0:T(1,128)S(1)}, s32[1,1,512]{2,1,0:T(1,128)}, u32[]{:S(2)}) copy-start(s32[1,1,512]{2,1,0:T(1,128)} %param.22) | copy-start | bytes 6148
  100.0 1.0 copy-start

commit v4 on v3

--- a/solution.py
+++ b/solution.py
@@ -370,17 +370,23 @@
 def reduce_rows(rows, at):
     lines = [rows[a:a + 1, :] for a in range(8)]
     d = [[jnp.broadcast_to(lines[a][:, at + b:at + b + 1], (1, 128)) for b in range(8)] for a in range(8)]
-    for a in range(8):
-        inv = 1.0 / d[a][a]
-        lines[a] = lines[a] * inv
-        top = [None if b <= a else d[a][b] * inv for b in range(8)]
-        d[a] = top
+    for p in range(0, 8, 2):
+        q = p + 1
+        pp, pq, qp, qq = d[p][p], d[p][q], d[q][p], d[q][q]
+        scale = 1.0 / (pp * qq - pq * qp)
+        pp, pq, qp, qq = qq * scale, pq * scale, qp * scale, pp * scale
+        lines[p], lines[q] = pp * lines[p] - pq * lines[q], qq * lines[q] - qp * lines[p]
+        later = range(q + 1, 8)
+        top = {b: (pp * d[p][b] - pq * d[q][b], qq * d[q][b] - qp * d[p][b]) for b in later}
         for c in range(8):
-            if c == a:
+            if c in (p, q):
                 continue
-            f = d[c][a]
-            lines[c] = lines[c] - f * lines[a]
-            d[c] = [d[c][b] if b <= a else d[c][b] - f * top[b] for b in range(8)]
+            f, g = d[c][p], d[c][q]
+            lines[c] = lines[c] - (f * lines[p] + g * lines[q])
+            for b in later:
+                d[c][b] = d[c][b] - (f * top[b][0] + g * top[b][1])
+        for b in later:
+            d[p][b], d[q][b] = top[b]
     return lines
 
 
@@ -449,7 +455,7 @@
         for k in range(8):
             acc = acc + jnp.where(row == i * 8 + k, part[k * 16:(k + 1) * 16, :], 0.0)
         return acc
-    picked = lax.fori_loop(0, 9, gather, jnp.zeros((16, 512), F32))
+    picked = lax.fori_loop(0, 9, gather, jnp.zeros((16, 512), F32), unroll=True)
     mod = mod_ref[...]
     hi = mod.astype(BF16)
     rest = mod - hi.astype(F32)

time: 121 us -> 118 us (0.975)
  Pallas kernels: 118 us -> 115 us
    pallas_call x1, Pallas kernels: 18.7 us -> 15.6 us  [analysis(): pl.pallas_call(analysis_kernel, out_shape=jax.ShapeDtypeStruct((16, 9216)...]
where the time goes in v4:
time: 118 us; the launch traced here: 117 us
  Pallas kernels  115 us (97%)
    pallas_call x1, Pallas kernels, forecast(): pl.pallas_call(forecast_kernel, out_shape=jax.ShapeDtypeStruct((GROUP, 72...  99.2 us
    pallas_call x1, Pallas kernels, analysis(): pl.pallas_call(analysis_kernel, out_shape=jax.ShapeDtypeStruct((16, 9216)...  15.6 us

profile of v4, /device:TPU:56, one launch (start us, length us, event | category | flops | bytes accessed | tf_op | source)
XLA Modules:
  0.0 116.5 jit_solution(14277118034365029956)
XLA Ops:
  0.0 0.0 copy-start.1
  0.0 0.0 copy-start.4
  0.0 0.0 copy-start.3
  0.0 0.0 copy-start.2
  0.7 99.2 %forecast.1.tile_ref = bf16[16,72,128]{2,1,0:T(8,128)(2,1)} custom-call(bf16[6,64,384]{2,1,0:T(8,128)(2,1)} %bitcast.13, bf16[64,128]{1,0:T(8,128)(2,1)} %bitcast.14, bf16[2,2,128,128]{3,2,1,0:T(8,128)(2,1)} %spec_hbm.1, f32[2,128]{1,0:T(2,128)} %gain_hbm.1, bf16[2,256,128]{2,1,0:T(8,128)(2,1)} %up_hbm.1, bf16[2,128,256]{2,1,0:T(8,128)(2,1)} %down_hbm.1, ...), custom_call_target="tpu_custom_call" | custom-call | tf_op jit(solution)/shard_map/forecast/pallas_call | solution.py:340
  99.9 0.0 copy-done.1
  99.9 0.0 copy-done.4
  100.0 0.0 copy-done.3
  100.0 0.0 copy-done.2
  100.0 0.0 copy-start
  100.0 1.0 copy-done
  100.9 15.6 %analysis.1 = bf16[16,9216]{1,0:T(8,128)(2,1)} custom-call(bf16[16,72,128]{2,1,0:T(8,128)(2,1)S(1)} %copy-done, s32[1,1]{1,0:T(1,128)S(6)} %copy.16.count_ref, s32[1,512]{1,0:T(1,128)S(1)} %bitcast.10, f32[1,512]{1,0:T(1,128)S(1)} %bitcast.11, f32[1,512]{1,0:T(1,128)S(1)} %bitcast.12, f32[16,144]{1,0:T(8,128)S(1)} %bitcast.9), custom_call_target="tpu_custom_call" | custom-call | tf_op jit(solution)/shard_map/analysis/pallas_call | solution.py:502
Async XLA Ops:
  0.0 99.9 %copy-start.1 = (f32[1,1,16,144]{3,2,1,0:T(8,128)S(1)}, f32[1,1,16,144]{3,2,1,0:T(8,128)}, u32[]{:S(2)}) copy-start(f32[1,1,16,144]{3,2,1,0:T(8,128)} %param.26) | copy-start | bytes 27652
  0.0 99.9 %copy-start.4 = (f32[1,1,512]{2,1,0:T(1,128)S(1)}, f32[1,1,512]{2,1,0:T(1,128)}, u32[]{:S(2)}) copy-start(f32[1,1,512]{2,1,0:T(1,128)} %param.25) | copy-start | bytes 6148
  0.0 100.0 %copy-start.3 = (f32[1,1,512]{2,1,0:T(1,128)S(1)}, f32[1,1,512]{2,1,0:T(1,128)}, u32[]{:S(2)}) copy-start(f32[1,1,512]{2,1,0:T(1,128)} %param.24) | copy-start | bytes 6148
  0.0 100.0 %copy-start.2 = (s32[1,1,512]{2,1,0:T(1,128)S(1)}, s32[1,1,512]{2,1,0:T(1,128)}, u32[]{:S(2)}) copy-start(s32[1,1,512]{2,1,0:T(1,128)} %param.22) | copy-start | bytes 6148
  100.0 1.0 copy-start

commit v5 on v4

--- a/solution.py
+++ b/solution.py
@@ -134,7 +134,15 @@
 
         def finish(self, half):
             def body(d, _):
-                self.copy(half, d).wait()
+                self.copy(half, d).wait_recv()
+                return 0
+
+            lax.fori_loop(0, SUB - 1, body, 0)
+
+        def drain(self):
+            def body(d, _):
+                self.copy(0, d).wait_send()
+                self.copy(1, d).wait_send()
                 return 0
 
             lax.fori_loop(0, SUB - 1, body, 0)
@@ -328,6 +336,8 @@
 
     own = pltpu.make_async_copy(tiles.at[group], out_ref.at[group], local_sem.at[10])
     own.start()
+    for done in (first, second, third, fourth):
+        done.drain()
     own.wait()
     lax.fori_loop(1, GROUP, tile_finish, 0)
 

time: 118 us -> 117 us (level)
  no operation moved by 1% of the time
where the time goes in v5:
time: 117 us; the launch traced here: 116 us
  Pallas kernels  114 us (97%)
    pallas_call x1, Pallas kernels, forecast(): pl.pallas_call(forecast_kernel, out_shape=jax.ShapeDtypeStruct((GROUP, 72...  98.9 us
    pallas_call x1, Pallas kernels, analysis(): pl.pallas_call(analysis_kernel, out_shape=jax.ShapeDtypeStruct((16, 9216)...  15.6 us

profile of v5, /device:TPU:56, one launch (start us, length us, event | category | flops | bytes accessed | tf_op | source)
XLA Modules:
  0.0 116.2 jit_solution(8593678303878280771)
XLA Ops:
  0.0 0.0 copy-start.1
  0.0 0.0 copy-start.4
  0.0 0.0 copy-start.3
  0.0 0.0 copy-start.2
  0.7 98.9 %forecast.1.tile_ref = bf16[16,72,128]{2,1,0:T(8,128)(2,1)} custom-call(bf16[6,64,384]{2,1,0:T(8,128)(2,1)} %bitcast.13, bf16[64,128]{1,0:T(8,128)(2,1)} %bitcast.14, bf16[2,2,128,128]{3,2,1,0:T(8,128)(2,1)} %spec_hbm.1, f32[2,128]{1,0:T(2,128)} %gain_hbm.1, bf16[2,256,128]{2,1,0:T(8,128)(2,1)} %up_hbm.1, bf16[2,128,256]{2,1,0:T(8,128)(2,1)} %down_hbm.1, ...), custom_call_target="tpu_custom_call" | custom-call | tf_op jit(solution)/shard_map/forecast/pallas_call | solution.py:350
  99.6 0.0 copy-done.1
  99.6 0.0 copy-done.4
  99.6 0.0 copy-done.3
  99.6 0.0 copy-done.2
  99.7 0.0 copy-start
  99.7 1.0 copy-done
  100.6 15.6 %analysis.1 = bf16[16,9216]{1,0:T(8,128)(2,1)} custom-call(bf16[16,72,128]{2,1,0:T(8,128)(2,1)S(1)} %copy-done, s32[1,1]{1,0:T(1,128)S(6)} %copy.16.count_ref, s32[1,512]{1,0:T(1,128)S(1)} %bitcast.10, f32[1,512]{1,0:T(1,128)S(1)} %bitcast.11, f32[1,512]{1,0:T(1,128)S(1)} %bitcast.12, f32[16,144]{1,0:T(8,128)S(1)} %bitcast.9), custom_call_target="tpu_custom_call" | custom-call | tf_op jit(solution)/shard_map/analysis/pallas_call | solution.py:512
Async XLA Ops:
  0.0 99.6 %copy-start.1 = (f32[1,1,16,144]{3,2,1,0:T(8,128)S(1)}, f32[1,1,16,144]{3,2,1,0:T(8,128)}, u32[]{:S(2)}) copy-start(f32[1,1,16,144]{3,2,1,0:T(8,128)} %param.26) | copy-start | bytes 27652
  0.0 99.6 %copy-start.4 = (f32[1,1,512]{2,1,0:T(1,128)S(1)}, f32[1,1,512]{2,1,0:T(1,128)}, u32[]{:S(2)}) copy-start(f32[1,1,512]{2,1,0:T(1,128)} %param.25) | copy-start | bytes 6148
  0.0 99.6 %copy-start.3 = (f32[1,1,512]{2,1,0:T(1,128)S(1)}, f32[1,1,512]{2,1,0:T(1,128)}, u32[]{:S(2)}) copy-start(f32[1,1,512]{2,1,0:T(1,128)} %param.24) | copy-start | bytes 6148
  0.0 99.6 %copy-start.2 = (s32[1,1,512]{2,1,0:T(1,128)S(1)}, s32[1,1,512]{2,1,0:T(1,128)}, u32[]{:S(2)}) copy-start(s32[1,1,512]{2,1,0:T(1,128)} %param.22) | copy-start | bytes 6148
  99.7 1.0 copy-start
